TPU v7x, 32 devices: a whole 2x2x4 slice. The times are simulated.
32 devices in a mesh: space: 4 (over x, core), freq: 8 (over z, y).
Axes of the slice: x: 2, y: 2, z: 4, core: 2. Of those that a mesh axis runs over, the one named last changes fastest.
Arguments:
- spectrum: float32 [32, 36, 128, 256], P('freq', None, 'space'), may hold values from 0.05 to 2
- land_sea: int32 [128, 256], P('space'), may hold values 0 or 1
- courant: float32 [32], P('freq'), may hold values from 0.2 to 0.65
- refract: float32 [32], P('freq'), may hold values from 0.2 to 0.9
- depth_dx: float32 [128, 256], P('space'), may hold values from -0.5 to 0.5
- depth_dy: float32 [128, 256], P('space'), may hold values from -0.5 to 0.5
- w_in: bfloat16 [1152, 2048], P(None, 'freq'), may hold values from -0.1875 to 0.1875
- w_out: bfloat16 [2048, 1152], P('freq'), may hold values from -0.125 to 0.125
Outputs:
- spectrum_out: float32 [32, 36, 128, 256], P('freq', None, 'space')
All inputs are finite; a program needn't handle non-finite values. No bound on the sum of `land_sea` on one device may be relied on, other than what follows from the above.
Results may differ from a plain program's by a relative error of at most 0.003.
Values may be sent and summed in bfloat16 or wider, within the bound.
No kernel may reach another device: no remote copies, remote signals or barrier semaphores. Data moves between devices by JAX's collectives and lax.ppermute only.
A program may use at most 128 MiB of HBM per device.

v0:
```python
import math

import jax
import jax.numpy as jnp
from jax import lax
from jax.experimental import pallas as pl
from jax.experimental.pallas import tpu as pltpu
from jax.sharding import PartitionSpec as P


DIRS = 36
STEP_SCALE = 0.5
EPSILON = 1e-06
ROOT_MAX = 2.9
ENCODE = 32767.0 / ROOT_MAX
DECODE = ROOT_MAX / 32767.0
NCOEF = 5
BLOCK = 2 * DIRS
f32, bf16, i16, i32 = jnp.float32, jnp.bfloat16, jnp.int16, jnp.int32


def encode(value):
    return (jnp.sqrt(value) * ENCODE + 0.5).astype(i32).astype(i16)


def decode(code):
    root = code.astype(i32).astype(f32) * DECODE
    return root * root


def device_of(position, space, groups):
    flipped = position + (space & 1) * (groups - 1 - 2 * position)
    return flipped ^ ((flipped >> 1) & 1) if groups % 4 == 0 else flipped


def position_of(device, space, groups):
    flipped = device ^ ((device >> 1) & 1) if groups % 4 == 0 else device
    return flipped + (space & 1) * (groups - 1 - 2 * flipped)


def spread(numbers_ref, row, angle_ref, wide_ref, at):
    cosine, sine = angle_ref[0], angle_ref[1]
    second = lax.broadcasted_iota(i32, (BLOCK, 128), 0) >= DIRS
    courant = jnp.where(second, numbers_ref[0, row + 1], numbers_ref[0, row])
    refract = jnp.where(second, numbers_ref[1, row + 1], numbers_ref[1, row])
    sx, sy = courant * cosine, courant * sine
    sx, sy = jnp.abs(sx), jnp.abs(sy)
    values = [1.0 - sx - sy, sx, sy, refract * sine, refract * cosine]
    for k, value in enumerate(values):
        wide_ref[k, pl.ds(at, BLOCK), :] = value


def one_sided(positive, row, yes, no):
    if all(positive):
        return yes()
    if not any(positive):
        return no()
    change = next(n for n in range(8) if positive[n] != positive[0])
    first, second = (yes(), no()) if positive[0] else (no(), yes())
    return jnp.where(row < change, first, second)


def transport(at, here, above, below, coefw, dx, dy, sea, write):
    cols = dx.shape[1]
    row = lax.broadcasted_iota(i32, (8, cols), 0)
    lane = lax.broadcasted_iota(i32, (8, cols), 1)
    count = BLOCK // 8
    cosine = [math.cos((d + 0.5) * (2.0 * math.pi / DIRS)) > 0 for d in range(DIRS)] * 2
    sine = [math.sin((d + 0.5) * (2.0 * math.pi / DIRS)) > 0 for d in range(DIRS)] * 2
    part = [pl.ds(pl.multiple_of(at + g * 8, 8), 8) for g in range(count)]
    shifted, forward, backward = [], [], []
    for g in range(count):
        center = here(part[g])
        rows = slice(g * 8, g * 8 + 8)
        beside = one_sided(cosine[rows], row, lambda: above(part[g]), lambda: below(part[g]))
        behind = one_sided(
            sine[rows],
            row,
            lambda: jnp.where(lane == 0, 0.0, pltpu.roll(center, 1, 1)),
            lambda: jnp.where(lane == cols - 1, 0.0, pltpu.roll(center, cols - 1, 1)),
        )
        keep, sx, sy, turn_x, turn_y = (
            jnp.concatenate([coefw[k, part[g], :]] * (cols // 128), axis=1) for k in range(NCOEF)
        )
        value = center * keep + beside * sx + behind * sy
        turning = (turn_x * dx - turn_y * dy) * value
        forward.append(jnp.maximum(turning, 0.0))
        backward.append(forward[g] - turning)
        shifted.append(value - jnp.abs(turning))
    down = [pltpu.roll(value, 1, 0) for value in forward]
    up = [pltpu.roll(value, 7, 0) for value in backward]
    half = DIRS // 8
    for g in range(count):
        before = pltpu.roll(forward[half], 5, 0) if g == 0 else down[g - 1]
        after = pltpu.roll(backward[half], 3, 0) if g == count - 1 else up[g + 1]
        moved = jnp.where(row == 0, before, down[g])
        other = jnp.where(row == 7, after, up[g])
        if g == half:
            moved = jnp.where(row == DIRS % 8, pltpu.roll(forward[count - 1], 5, 0), moved)
            other = jnp.where(row == DIRS % 8 - 1, pltpu.roll(backward[0], 3, 0), other)
        write(part[g], (shifted[g] + moved + other) * sea)


def first_kernel(split, groups, prows, where_ref, numbers_ref, source_ref, low_ref, high_ref, dx_ref, dy_ref, sea_ref, *refs):
    outs, (spec_ref, shifted_ref, turning_ref, sem) = refs[: len(split) * groups], refs[len(split) * groups :]
    channels, cols = low_ref.shape
    rows = groups * prows
    space, device = where_ref[0], where_ref[1]
    line = lax.broadcasted_iota(i32, (rows, cols), 0)
    lane = lax.broadcasted_iota(i32, (rows, cols), 1)
    angles = [(d + 0.5) * (2.0 * math.pi / DIRS) for d in range(DIRS)]

    def copy(f):
        part = pl.ds(pl.multiple_of(f * (DIRS * rows), 8), DIRS * rows)
        return pltpu.make_async_copy(source_ref.at[part, :], spec_ref.at[part, :], sem.at[f])

    for f in range(channels // DIRS):
        copy(f).start()

    @pl.loop(0, channels // DIRS)
    def _(f):
        copy(f).wait()
        courant, refract = numbers_ref[0, f], numbers_ref[1, f]
        dx, dy = dx_ref[...] * refract, dy_ref[...] * refract
        for d in range(DIRS):
            c = f * DIRS + d
            cosine, sine = math.cos(angles[d]), math.sin(angles[d])
            center = spec_ref[pl.ds(pl.multiple_of(c * rows, 8), rows), :]
            if cosine > 0:
                beside = jnp.where(line == 0, low_ref[pl.ds(c, 1), :], pltpu.roll(center, 1, 0))
            else:
                beside = jnp.where(line == rows - 1, high_ref[pl.ds(c, 1), :], pltpu.roll(center, rows - 1, 0))
            if sine > 0:
                behind = jnp.where(lane == 0, 0.0, pltpu.roll(center, 1, 1))
            else:
                behind = jnp.where(lane == cols - 1, 0.0, pltpu.roll(center, cols - 1, 1))
            sx, sy = courant * abs(cosine), courant * abs(sine)
            shifted = center * (1.0 - sx - sy) + beside * sx + behind * sy
            shifted_ref[c] = shifted
            turning_ref[c] = (sine * dx - cosine * dy) * shifted

    some = 16 if channels % 16 == 0 else 8

    share = 8 // prows

    for tile_at in range(0, groups, share):
        t = position_of(tile_at ^ device, space, groups) // share
        tall = pl.ds(pl.multiple_of(t * 8, 8), 8)
        slots = [(device_of(t * share + i, space, groups) ^ device) - tile_at for i in range(share)]

        @pl.loop(0, channels // some)
        def _(n):
            at = pl.multiple_of(n * some, some)
            for h in range(cols // 128):
                lanes = pl.ds(h * 128, 128)
                sea = sea_ref[tall, lanes].astype(f32)
                tile = []
                for i in range(some):
                    c = at + i
                    d = c % DIRS
                    before = turning_ref[jnp.where(d == 0, c + DIRS - 1, c - 1), tall, lanes]
                    after = turning_ref[jnp.where(d == DIRS - 1, c - DIRS + 1, c + 1), tall, lanes]
                    value = shifted_ref[c, tall, lanes] - jnp.abs(turning_ref[c, tall, lanes])
                    tile.append((value + jnp.maximum(before, 0.0) - jnp.minimum(after, 0.0)) * sea)
                tile = encode(jnp.swapaxes(jnp.stack(tile), 0, 1))
                for slot in range(share):
                    for j in range(prows):
                        value = tile[j]
                        for i in range(1, share):
                            value = jnp.where(slots[i] == slot, tile[i * prows + j], value)
                        for m, members in enumerate(split):
                            if j in members:
                                out = outs[m * groups + tile_at + slot]
                                out[members.index(j), pl.ds(at, some), lanes] = value


class Net:
    def __init__(self, plan, groups, spaces, space, parts, scratch):
        self.x, self.hid, self.win, self.wout, self.sem = scratch
        self.groups, self.spaces = groups, spaces
        self.hidden, self.channels = self.win.shape
        self.hpart = self.hidden // (groups * spaces)
        self.cpart = self.channels // spaces
        self.pending = True
        pieces = [(kind, f, s, part.at[n]) for part, (kind, places) in zip(parts, plan) for n, (f, s) in enumerate(places)]
        for kind, f, s, piece in sorted(pieces, key=lambda item: item[:3]):
            self.copy(kind, f, space ^ s, piece).start()
        self.piece = [part.at[0] for part in (parts[0], parts[-1])]

    def copy(self, kind, f, s, piece):
        if kind == 0:
            size, unit = self.hpart, f * self.spaces + s
            target = self.win.at[pl.ds(pl.multiple_of(unit * size, 8), size), :]
        else:
            size, unit = self.cpart, s * self.groups + f
            width = self.hidden // self.groups
            target = self.wout.at[pl.ds(pl.multiple_of(s * size, 8), size), pl.ds(f * width, width)]
        return pltpu.make_async_copy(piece.at[pl.ds(0, size), :], target, self.sem.at[kind, unit])

    def run(self, inverse, emit):
        mblock, cblock = min(512, self.hidden), 4 * BLOCK
        for m in range(0, self.hidden, mblock):
            if self.pending and m == 0:
                for unit in range(self.groups * self.spaces):
                    self.copy(0, unit // self.spaces, unit % self.spaces, self.piece[0]).wait()
            pre = jnp.dot(self.win[m : m + mblock, :], self.x[...], preferred_element_type=f32) * inverse
            half = 0.5 * pre
            inside = pre * (0.7978845608028654 + (0.7978845608028654 * 0.044715) * (pre * pre))
            self.hid[m : m + mblock, :] = (half + half * jnp.tanh(inside)).astype(bf16)
        for c in range(0, self.channels, cblock):
            if self.pending and c == 0:
                for s in range(self.spaces):
                    for f in range(self.groups):
                        self.copy(1, f, s, self.piece[1]).wait()
            source = jnp.dot(self.wout[c : c + cblock, :], self.hid[...], preferred_element_type=f32)
            emit(pl.ds(c, cblock), jnp.exp(STEP_SCALE * jnp.tanh(source)))
        self.pending = False


def mean_inverse(total, channels):
    total = jnp.sum(total, axis=0, keepdims=True)
    return 1.0 / (total * (1.0 / channels) + EPSILON)


def step_one(own, codes, field_ref, device, net):
    local, cols = codes[0].shape[1:]
    for n in range(len(own)):
        total = jnp.zeros((8, cols), f32)
        for k in range(len(codes)):
            row = (k ^ device) * local
            for b in range(local // BLOCK):
                value = decode(codes[k][n, pl.ds(b * BLOCK, BLOCK), :])
                field_ref[n, pl.ds(pl.multiple_of(row + b * BLOCK, 8), BLOCK), :] = value
                total = total + jnp.sum(value.reshape(BLOCK // 8, 8, cols), axis=0)
        net.x[...] = field_ref[n].astype(bf16)

        def emit(part, factor):
            field_ref[n, part, :] = field_ref[n, part, :] * factor

        net.run(mean_inverse(total, net.channels), emit)


def step_two(own, held, outs, grid, coefw, moved_ref, first_row, device, net):
    numbers_ref, angle_ref, dx_ref, dy_ref, sea_ref = grid
    local, cols = outs[0].shape[1:]
    groups, channels = len(outs), net.channels

    @pl.loop(0, groups)
    def _(q):
        row = (q ^ device) * (local // DIRS)
        for b in range(local // BLOCK):
            at = pl.multiple_of(q * local + b * BLOCK, 8)
            spread(numbers_ref, row + 2 * b, angle_ref, coefw, at)

    for n, j in enumerate(own):
        r = first_row + j
        dx, dy = dx_ref[pl.ds(r, 1), :], dy_ref[pl.ds(r, 1), :]
        sea = sea_ref[pl.ds(r, 1), :].astype(f32)
        (here, hn), (above, an), (below, bn) = held(j), held(j - 1), held(j + 1)

        def block(b, total):
            sums = [total]

            def write(part, value):
                moved_ref[part, :] = value
                sums.append(sums[-1] + value)

            at = pl.multiple_of(b * BLOCK, 8)
            transport(
                at,
                lambda part: here[hn, part, :],
                lambda part: above[an, part, :],
                lambda part: below[bn, part, :],
                coefw,
                jnp.broadcast_to(dx, (8, cols)),
                jnp.broadcast_to(dy, (8, cols)),
                jnp.broadcast_to(sea, (8, cols)),
                write,
            )
            return sums[-1]

        total = lax.fori_loop(0, channels // BLOCK, block, jnp.zeros((8, cols), f32))
        net.x[...] = moved_ref[...].astype(bf16)

        def emit(part, factor):
            moved_ref[part, :] = moved_ref[part, :] * factor

        net.run(mean_inverse(total, channels), emit)
        for k in range(groups):
            outs[k][n] = encode(moved_ref[pl.ds(pl.multiple_of((k ^ device) * local, 8), local), :])


def take(refs, count):
    return list(refs[:count]), refs[count:]


def outer_one_kernel(split, sizes, plan, where_ref, numbers_ref, angle_ref, *refs):
    groups, spaces, _ = sizes
    codes, refs = take(refs, groups)
    parts, refs = take(refs, len(plan))
    (field_ref, *edges), refs = take(refs, 3)
    net = Net(plan, groups, spaces, where_ref[0], parts, refs)
    step_one(split[0], codes, field_ref, where_ref[1], net)
    for edge, n in zip(edges, (0, len(split[0]) - 1)):
        edge[...] = encode(field_ref[n])


def inner_kernel(split, sizes, plan, where_ref, *refs):
    groups, spaces, prows = sizes
    grid, refs = take(refs, 5)
    (outer_ref,), refs = take(refs, 1)
    codes, refs = take(refs, groups)
    parts, refs = take(refs, len(plan))
    (field_ref,), refs = take(refs, 1)
    outs, refs = take(refs, groups)
    (moved_ref, coefw), scratch = take(refs, 2)
    space, device = where_ref[0], where_ref[1]
    net = Net(plan, groups, spaces, space, parts, scratch)
    step_one(split[1], codes, field_ref, device, net)

    def held(j):
        return (outer_ref, split[0].index(j)) if j in split[0] else (field_ref, split[1].index(j))

    first_row = position_of(device, space, groups) * prows
    step_two(split[1], held, outs, grid, coefw, moved_ref, first_row, device, net)


def outer_two_kernel(split, sizes, plan, where_ref, *refs):
    groups, spaces, prows = sizes
    grid, refs = take(refs, 5)
    fields, refs = take(refs, len(split))
    halos, refs = take(refs, 2)
    parts, refs = take(refs, len(plan))
    outs, refs = take(refs, groups)
    (halo_ref, moved_ref, coefw), scratch = take(refs, 3)
    space, device = where_ref[0], where_ref[1]
    net = Net(plan, groups, spaces, space, parts, scratch)
    for n, halo in enumerate(halos):
        halo_ref[n] = decode(halo[...])

    def held(j):
        if j < 0 or j >= prows:
            return halo_ref, int(j >= prows)
        for field, members in zip(fields, split):
            if j in members:
                return field, members.index(j)

    first_row = position_of(device, space, groups) * prows
    step_two(split[0], held, outs, grid, coefw, moved_ref, first_row, device, net)


def last_kernel(split, groups, prows, where_ref, *refs):
    codes, out_ref = refs[:-1], refs[-1]
    local, cols = codes[0].shape[1:]
    rows = groups * prows
    space, device = where_ref[0], where_ref[1]
    share = 8 // prows
    some = 16 if local % 16 == 0 else 8

    for tile_at in range(0, groups, share):
        t = position_of(tile_at ^ device, space, groups) // share
        slots = [(device_of(t * share + i, space, groups) ^ device) - tile_at for i in range(share)]

        @pl.loop(0, local // some)
        def _(n):
            at = pl.multiple_of(n * some, some)
            for h in range(cols // 128):
                lanes = pl.ds(h * 128, 128)
                tile = []
                for i in range(share):
                    for j in range(prows):
                        for m, members in enumerate(split):
                            if j in members:
                                source = codes[m * groups + tile_at : m * groups + tile_at + share]
                                found = [code[members.index(j), pl.ds(at, some), lanes] for code in source]
                        value = found[0]
                        for slot in range(1, share):
                            value = jnp.where(slots[i] == slot, found[slot], value)
                        tile.append(decode(value))
                tile = jnp.swapaxes(jnp.stack(tile), 0, 1)
                for k in range(some):
                    start = pl.multiple_of((at + k) * rows + t * 8, 8)
                    out_ref[pl.ds(start, 8), lanes] = tile[k]


def exchange(array, axis, bit):
    count = lax.axis_size(axis)
    return lax.ppermute(array, axis, [(i, i ^ bit) for i in range(count)])


def gather(piece, freq_bits, space_bits):
    have, places = piece[None], [(0, 0)]
    for bit in freq_bits[:-1]:
        have = jnp.concatenate([have, exchange(have, "freq", bit)], axis=0)
        places = places + [(f ^ bit, s) for f, s in places]
    arrays = [(have, places)]
    for bit in freq_bits[-1:]:
        arrays.append((exchange(have, "freq", bit), [(f ^ bit, s) for f, s in places]))
    for n, bit in enumerate(space_bits):
        got = []
        for have, places in arrays:
            flip = [(f, s ^ bit) for f, s in places]
            got.append((exchange(have, "space", bit), flip))
        if n == 0 or n == len(space_bits) - 1:
            arrays = arrays + got
        else:
            arrays = [
                (jnp.concatenate([a, b], axis=0), p + q) for (a, p), (b, q) in zip(arrays, got)
            ]
    return arrays


def bits_of(count):
    return [1 << n for n in reversed(range(count.bit_length() - 1))]


def split3(value):
    high = lax.reduce_precision(value, 8, 7)
    rest = value - high
    middle = lax.reduce_precision(rest, 8, 7)
    return [part.astype(bf16) for part in (high, middle, rest - middle)]


def body(spectrum, land_sea, courant, refract, depth_dx, depth_dy, w_in, w_out):
    groups, spaces = lax.axis_size("freq"), lax.axis_size("space")
    space, freq = lax.axis_index("space"), lax.axis_index("freq")
    freqs, dirs, rows, cols = spectrum.shape
    local = freqs * dirs
    channels = local * groups
    prows = rows // groups
    hidden_local = w_in.shape[1]
    hidden = hidden_local * groups

    last = spectrum[:, :, rows - 1, :].reshape(local, cols)
    first = spectrum[:, :, 0, :].reshape(local, cols)
    up = [(i, i + 1) for i in range(spaces - 1)]
    low = lax.ppermute(last, "space", up)
    high = lax.ppermute(first, "space", [(b, a) for a, b in up])

    hpart, cpart = hidden_local // spaces, channels // spaces
    win_piece = lax.dynamic_slice_in_dim(w_in, space * hpart, hpart, 1).T
    numbers = jnp.stack(split3(courant) + split3(refract))
    numbers = jnp.pad(numbers, ((0, 2), (0, channels - freqs)))
    win_piece = jnp.concatenate([win_piece, numbers], axis=0)
    wout_piece = lax.dynamic_slice_in_dim(w_out, space * cpart, cpart, 1).T
    win_arrays = gather(win_piece, bits_of(groups), bits_of(spaces))
    wout_arrays = gather(wout_piece, bits_of(groups), bits_of(spaces))
    plan, parts = [], []
    for kind, arrays in ((0, win_arrays), (1, wout_arrays)):
        for have, places in arrays:
            plan.append((kind, places))
            parts.append(have)
    found = {}
    for have, places in win_arrays[:2]:
        raw = have[:, hpart : hpart + 6, 0:freqs].astype(f32)
        raw = raw.reshape(len(places), 2, 3, freqs).sum(axis=2)
        found.update({f: raw[n] for n, (f, s) in enumerate(places)})
    numbers = jnp.concatenate([found[f] for f in range(groups)], axis=1)

    angles = (jnp.arange(DIRS, dtype=f32) + 0.5) * (2.0 * math.pi / DIRS)
    angles = jnp.stack([jnp.cos(angles), jnp.sin(angles)])
    angles = jnp.broadcast_to(jnp.tile(angles, (1, 2))[:, :, None], (2, BLOCK, 128))
    place = jnp.stack([space, freq]).astype(i32)

    any_spec = pl.BlockSpec(memory_space=pl.ANY)
    vmem = pl.BlockSpec(memory_space=pltpu.VMEM)
    smem = pl.BlockSpec(memory_space=pltpu.SMEM)
    params = pltpu.CompilerParams(vmem_limit_bytes=60 * 1024 * 1024)
    net_scratch = [
        pltpu.VMEM((channels, cols), bf16),
        pltpu.VMEM((hidden, cols), bf16),
        pltpu.VMEM((hidden, channels), bf16),
        pltpu.VMEM((channels, hidden), bf16),
        pltpu.SemaphoreType.DMA((2, groups * spaces)),
    ]

    outer = sorted({0, prows - 1})
    inner = [j for j in range(prows) if j not in outer]
    split = [outer] + ([inner] if inner else [])

    def code_shapes(own):
        return [jax.ShapeDtypeStruct((len(own), local, cols), i16)] * groups

    order = sorted(range(1, groups), key=lambda k: -k)

    def transpose(parts):
        arrived = list(parts)
        for k in order:
            arrived[k] = exchange(parts[k], "freq", k)
        return arrived

    flat = spectrum.reshape(local * rows, cols)
    sent = pl.pallas_call(
        lambda *refs: first_kernel(split, groups, prows, *refs),
        in_specs=[smem, smem, any_spec] + [vmem] * 5,
        out_specs=[vmem] * (len(split) * groups),
        out_shape=[shape for own in split for shape in code_shapes(own)],
        scratch_shapes=[pltpu.VMEM((local * rows, cols), f32)]
        + [pltpu.VMEM((local, rows, cols), f32)] * 2
        + [pltpu.SemaphoreType.DMA((freqs,))],
        compiler_params=params,
        name="kfirst",
    )(place, jnp.stack([courant, refract]), flat, low, high, depth_dx, depth_dy, land_sea)
    arrived = [transpose(sent[n * groups : (n + 1) * groups]) for n in range(len(split))]

    sizes = (groups, spaces, prows)
    step_scratch = [pltpu.VMEM((channels, cols), f32), pltpu.VMEM((NCOEF, channels, 128), f32)]

    def field_shape(own):
        return jax.ShapeDtypeStruct((len(own), channels, cols), f32)

    edge_shape = jax.ShapeDtypeStruct((channels, cols), i16)
    field, *edge = pl.pallas_call(
        lambda *refs: outer_one_kernel(split, sizes, plan, *refs),
        in_specs=[smem, smem, any_spec] + [vmem] * groups + [any_spec] * len(plan),
        out_specs=[vmem] * 3,
        out_shape=[field_shape(outer), edge_shape, edge_shape],
        scratch_shapes=net_scratch,
        compiler_params=params,
        name="kone0",
    )(place, numbers, angles, *arrived[0], *parts)
    fields = [field]

    chain = []
    for n in range(spaces * groups):
        s, p = divmod(n, groups)
        chain.append(s * groups + device_of(p, s, groups))
    chain = list(zip(chain[:-1], chain[1:]))
    low = lax.ppermute(edge[1], ("space", "freq"), chain)
    high = lax.ppermute(edge[0], ("space", "freq"), [(b, a) for a, b in chain])

    grid = (numbers, angles, depth_dx, depth_dy, land_sea)
    back = []
    if inner:
        field, *sent = pl.pallas_call(
            lambda *refs: inner_kernel(split, sizes, plan, *refs),
            in_specs=[smem, smem] + [vmem] * (5 + groups) + [any_spec] * len(plan),
            out_specs=[vmem] * (1 + groups),
            out_shape=[field_shape(inner)] + code_shapes(inner),
            scratch_shapes=step_scratch + net_scratch,
            compiler_params=params,
            name="kmid",
        )(place, *grid, fields[0], *arrived[1], *parts)
        fields.append(field)
        back = transpose(sent)
    sent = pl.pallas_call(
        lambda *refs: outer_two_kernel(split, sizes, plan, *refs),
        in_specs=[smem, smem] + [vmem] * (4 + len(split) + 2) + [any_spec] * len(plan),
        out_specs=[vmem] * groups,
        out_shape=code_shapes(outer),
        scratch_shapes=[pltpu.VMEM((2, channels, cols), f32)] + step_scratch + net_scratch,
        compiler_params=params,
        name="ktwo0",
    )(place, *grid, *fields, low, high, *parts)
    back = transpose(sent) + back

    out = pl.pallas_call(
        lambda *refs: last_kernel(split, groups, prows, *refs),
        in_specs=[smem] + [vmem] * (len(split) * groups),
        out_specs=vmem,
        out_shape=jax.ShapeDtypeStruct((local * rows, cols), f32),
        compiler_params=params,
        name="klast",
    )(place, *back)
    return out.reshape(freqs, dirs, rows, cols)


def solution(mesh):
    placed = (
        P("freq", None, "space", None),
        P("space", None),
        P("freq"),
        P("freq"),
        P("space", None),
        P("space", None),
        P(None, "freq"),
        P("freq", None),
    )

    return jax.shard_map(
        body, mesh=mesh, in_specs=placed, out_specs=P("freq", None, "space", None), check_vma=False
    )
```

profile of v0, /device:TPU:0, one launch (start us, length us, event | category | flops | bytes accessed | tf_op | source)
XLA Modules:
  0.0 278.0 jit_solution(15560946838303099981)
XLA Ops:
  1.3 4.1 %collective-permute-start.18 = (bf16[1,288,256]{2,1,0:T(8,128)(2,1)S(1)}, bf16[1,288,256]{2,1,0:T(8,128)(2,1)S(1)}, u32[]{:S(2)}, u32[]{:S(2)}) collective-permute-start(bf16[1,288,256]{2,1,0:T(8,128)(2,1)S(1)} %bitcast.35), channel_id=1, source_target_pairs={{0,4},{1,5},{2,6},{3,7},{4,0},{5,1},{6,2},{7,3},{8,12},{9,13},{10,... | collective-permute-start | bytes 442376 | tf_op jit(solution)/shard_map/ppermute | solution.py:388
  12.8 6.8 %collective-permute-done = bf16[1,72,1152]{2,1,0:T(8,128)(2,1)S(1)} collective-permute-done((bf16[1,72,1152]{2,1,0:T(8,128)(2,1)S(1)}, bf16[1,72,1152]{2,1,0:T(8,128)(2,1)S(1)}, u32[]{:S(2)}, u32[]{:S(2)}) %collective-permute-start) | collective-permute-done | bytes 165920 | tf_op jit(solution)/shard_map/ppermute | solution.py:388
  24.4 11.9 %kfirst.1 = (s16[2,144,256]{2,1,0:T(8,128)(2,1)}, s16[2,144,256]{2,1,0:T(8,128)(2,1)}, s16[2,144,256]{2,1,0:T(8,128)(2,1)}, s16[2,144,256]{2,1,0:T(8,128)(2,1)},...) custom-call(s32[2]{0:T(128)} %pad_add_fusion.refs_0_, ...), custom_call_target="tpu_custom_call" | custom-call | tf_op jit(solution)/shard_map/kfirst/pallas_call | solution.py:493
  52.6 6.7 %collective-permute-done.9.refs_8_ = s16[2,144,256]{2,1,0:T(8,128)(2,1)S(1)} collective-permute-done((s16[2,144,256]{2,1,0:T(8,128)(2,1)}, s16[2,144,256]{2,1,0:T(8,128)(2,1)S(1)}, u32[]{:S(2)}, u32[]{:S(2)}) %collective-permute-start.9) | collective-permute-done | bytes 147488 | tf_op jit(solution)/shard_map/ppermute | solution.py:388
  62.3 4.2 %collective-permute-done.10.refs_9_ = s16[2,144,256]{2,1,0:T(8,128)(2,1)S(1)} collective-permute-done((s16[2,144,256]{2,1,0:T(8,128)(2,1)}, s16[2,144,256]{2,1,0:T(8,128)(2,1)S(1)}, u32[]{:S(2)}, u32[]{:S(2)}) %collective-permute-start.10) | collective-permute-done | bytes 147488 | tf_op jit(solution)/shard_map/ppermute | solution.py:388
  66.5 4.3 %collective-permute-start.11 = (s16[2,144,256]{2,1,0:T(8,128)(2,1)}, s16[2,144,256]{2,1,0:T(8,128)(2,1)}, u32[]{:S(2)}, u32[]{:S(2)}) collective-permute-start(s16[2,144,256]{2,1,0:T(8,128)(2,1)} %get-tuple-element.48), channel_id=1, source_target_pairs={{0,7},{1,6},{2,5},{3,4},{4,3},{5,2},{6,1},{7,0},{8,15},{9,14},{10,... | collective-permute-start | bytes 442376 | tf_op jit(solution)/shard_map/ppermute | solution.py:388
  70.9 3.9 %collective-permute-done.11.refs_10_ = s16[2,144,256]{2,1,0:T(8,128)(2,1)} collective-permute-done((s16[2,144,256]{2,1,0:T(8,128)(2,1)}, s16[2,144,256]{2,1,0:T(8,128)(2,1)}, u32[]{:S(2)}, u32[]{:S(2)}) %collective-permute-start.11) | collective-permute-done | bytes 147488 | tf_op jit(solution)/shard_map/ppermute | solution.py:388
  80.5 12.2 %collective-permute-done.12.refs_13_.refs_17_.refs_12_ = bf16[4,72,1152]{2,1,0:T(8,128)(2,1)} collective-permute-done((bf16[4,72,1152]{2,1,0:T(8,128)(2,1)S(1)}, bf16[4,72,1152]{2,1,0:T(8,128)(2,1)}, u32[]{:S(2)}, u32[]{:S(2)}) %collective-permute-start.12) | collective-permute-done | bytes 663584 | tf_op jit(solution)/shard_map/ppermute | solution.py:388
  93.3 25.8 %collective-permute-done.22.refs_22_.refs_26_.refs_21_ = bf16[4,288,256]{2,1,0:T(8,128)(2,1)} collective-permute-done((bf16[4,288,256]{2,1,0:T(8,128)(2,1)}, bf16[4,288,256]{2,1,0:T(8,128)(2,1)}, u32[]{:S(2)}, u32[]{:S(2)}) %collective-permute-start.22) | collective-permute-done | bytes 589856 | tf_op jit(solution)/shard_map/ppermute | solution.py:388
  123.2 12.9 %kone0.1 = (f32[2,1152,256]{2,1,0:T(8,128)}, s16[1152,256]{1,0:T(8,128)(2,1)}, s16[1152,256]{1,0:T(8,128)(2,1)}) custom-call(s32[2]{0:T(128)} %pad_add_fusion.refs_0_, f32[2,32]{1,0:T(2,128)} %concatenate.23.refs_1_, f32[2,72,128]{2,1,0:T(8,128)} %broadcast_in_dim.12.refs_2_, s16[2,144,256]{2,1,0:T(8,128)(2,1)} %get-tuple-element.41.refs_3_, ...), custom_call_target="tpu_custom_call" | custom-call | tf_op jit(solution)/shard_map/kone0/pallas_call | solution.py:513
  136.0 3.1 %collective-permute-start.34 = (s16[1152,256]{1,0:T(8,128)(2,1)}, s16[1152,256]{1,0:T(8,128)(2,1)S(1)}, u32[]{:S(2)}, u32[]{:S(2)}) collective-permute-start(s16[1152,256]{1,0:T(8,128)(2,1)} %get-tuple-element.59), channel_id=1, source_target_pairs={{0,1},{1,3},{3,2},{2,4},{4,5},{5,7},{7,6},{6,14},{14,15},{15,13},{... | collective-permute-start | bytes 1769480 | tf_op jit(solution)/shard_map/ppermute | solution.py:529
  142.6 4.0 %collective-permute-start.28 = (s16[2,144,256]{2,1,0:T(8,128)(2,1)S(1)}, s16[2,144,256]{2,1,0:T(8,128)(2,1)S(1)}, u32[]{:S(2)}, u32[]{:S(2)}) collective-permute-start(s16[2,144,256]{2,1,0:T(8,128)(2,1)S(1)} %copy-done.37), channel_id=1, source_target_pairs={{0,2},{1,3},{2,0},{3,1},{4,6},{5,7},{6,4},{7,5},{8,10},{9,11},{10,... | collective-permute-start | bytes 442376 | tf_op jit(solution)/shard_map/ppermute | solution.py:388
  146.8 11.8 %collective-permute-done.27.refs_8_ = s16[2,144,256]{2,1,0:T(8,128)(2,1)S(1)} collective-permute-done((s16[2,144,256]{2,1,0:T(8,128)(2,1)S(1)}, s16[2,144,256]{2,1,0:T(8,128)(2,1)S(1)}, u32[]{:S(2)}, u32[]{:S(2)}) %collective-permute-start.27) | collective-permute-done | bytes 147488 | tf_op jit(solution)/shard_map/ppermute | solution.py:388
  163.5 11.7 %collective-permute-done.30.refs_11_ = s16[2,144,256]{2,1,0:T(8,128)(2,1)S(1)} collective-permute-done((s16[2,144,256]{2,1,0:T(8,128)(2,1)}, s16[2,144,256]{2,1,0:T(8,128)(2,1)S(1)}, u32[]{:S(2)}, u32[]{:S(2)}) %collective-permute-start.30) | collective-permute-done | bytes 147488 | tf_op jit(solution)/shard_map/ppermute | solution.py:388
  176.2 3.6 %collective-permute-done.31.refs_12_ = s16[2,144,256]{2,1,0:T(8,128)(2,1)S(1)} collective-permute-done((s16[2,144,256]{2,1,0:T(8,128)(2,1)}, s16[2,144,256]{2,1,0:T(8,128)(2,1)S(1)}, u32[]{:S(2)}, u32[]{:S(2)}) %collective-permute-start.31) | collective-permute-done | bytes 147488 | tf_op jit(solution)/shard_map/ppermute | solution.py:388
  179.9 3.3 %collective-permute-done.33.refs_14_ = s16[2,144,256]{2,1,0:T(8,128)(2,1)S(1)} collective-permute-done((s16[2,144,256]{2,1,0:T(8,128)(2,1)}, s16[2,144,256]{2,1,0:T(8,128)(2,1)S(1)}, u32[]{:S(2)}, u32[]{:S(2)}) %collective-permute-start.33) | collective-permute-done | bytes 147488 | tf_op jit(solution)/shard_map/ppermute | solution.py:388
  183.8 25.0 %kmid.1 = (f32[2,1152,256]{2,1,0:T(8,128)}, s16[2,144,256]{2,1,0:T(8,128)(2,1)}, s16[2,144,256]{2,1,0:T(8,128)(2,1)}, s16[2,144,256]{2,1,0:T(8,128)(2,1)}, s16[2...) custom-call(s32[2]{0:T(128)} %pad_add_fusion.refs_0_, ...), custom_call_target="tpu_custom_call" | custom-call | tf_op jit(solution)/shard_map/kmid/pallas_call | solution.py:535
  211.2 3.9 %collective-permute-start.44 = (s16[2,144,256]{2,1,0:T(8,128)(2,1)}, s16[2,144,256]{2,1,0:T(8,128)(2,1)S(1)}, u32[]{:S(2)}, u32[]{:S(2)}) collective-permute-start(s16[2,144,256]{2,1,0:T(8,128)(2,1)} %get-tuple-element.71), channel_id=1, source_target_pairs={{0,2},{1,3},{2,0},{3,1},{4,6},{5,7},{6,4},{7,5},{8,10},{9,11},{10,... | collective-permute-start | bytes 442376 | tf_op jit(solution)/shard_map/ppermute | solution.py:388
  219.6 16.6 %ktwo0.1 = (s16[2,144,256]{2,1,0:T(8,128)(2,1)}, s16[2,144,256]{2,1,0:T(8,128)(2,1)}, s16[2,144,256]{2,1,0:T(8,128)(2,1)}, s16[2,144,256]{2,1,0:T(8,128)(2,1)}, ...) custom-call(s32[2]{0:T(128)} %pad_add_fusion.refs_0_, ...), custom_call_target="tpu_custom_call" | custom-call | tf_op jit(solution)/shard_map/ktwo0/pallas_call | solution.py:546
  244.9 5.4 %collective-permute-start.39 = (s16[2,144,256]{2,1,0:T(8,128)(2,1)}, s16[2,144,256]{2,1,0:T(8,128)(2,1)S(1)}, u32[]{:S(2)}, u32[]{:S(2)}) collective-permute-start(s16[2,144,256]{2,1,0:T(8,128)(2,1)} %get-tuple-element.65), channel_id=1, source_target_pairs={{0,4},{1,5},{2,6},{3,7},{4,0},{5,1},{6,2},{7,3},{8,12},{9,13},{10,... | collective-permute-start | bytes 442376 | tf_op jit(solution)/shard_map/ppermute | solution.py:388
  250.3 5.6 %collective-permute-start.40 = (s16[2,144,256]{2,1,0:T(8,128)(2,1)}, s16[2,144,256]{2,1,0:T(8,128)(2,1)S(1)}, u32[]{:S(2)}, u32[]{:S(2)}) collective-permute-start(s16[2,144,256]{2,1,0:T(8,128)(2,1)} %get-tuple-element.66), channel_id=1, source_target_pairs={{0,5},{1,4},{2,7},{3,6},{4,1},{5,0},{6,3},{7,2},{8,13},{9,12},{10,... | collective-permute-start | bytes 442376 | tf_op jit(solution)/shard_map/ppermute | solution.py:388
  259.6 8.0 %collective-permute-done.39.refs_5_ = s16[2,144,256]{2,1,0:T(8,128)(2,1)S(1)} collective-permute-done((s16[2,144,256]{2,1,0:T(8,128)(2,1)}, s16[2,144,256]{2,1,0:T(8,128)(2,1)S(1)}, u32[]{:S(2)}, u32[]{:S(2)}) %collective-permute-start.39) | collective-permute-done | bytes 147488 | tf_op jit(solution)/shard_map/ppermute | solution.py:388
  267.6 3.6 %collective-permute-done.40.refs_6_ = s16[2,144,256]{2,1,0:T(8,128)(2,1)S(1)} collective-permute-done((s16[2,144,256]{2,1,0:T(8,128)(2,1)}, s16[2,144,256]{2,1,0:T(8,128)(2,1)S(1)}, u32[]{:S(2)}, u32[]{:S(2)}) %collective-permute-start.40) | collective-permute-done | bytes 147488 | tf_op jit(solution)/shard_map/ppermute | solution.py:388
  272.0 6.0 %klast.1 = f32[4608,256]{1,0:T(8,128)} custom-call(s32[2]{0:T(128)} %pad_add_fusion.refs_0_, s16[2,144,256]{2,1,0:T(8,128)(2,1)} %get-tuple-element.61.refs_1_, s16[2,144,256]{2,1,0:T(8,128)(2,1)} %copy-done.15, s16[2,144,256]{2,1,0:T(8,128)(2,1)} %copy-done.16, s16[2,144,256]{2,1,0:T(8,128)(2,1)} %copy-done.17, s16[2,144,256]{2,1,0:T(8,128)(2,1)} %copy-done.18, ...), custom_call_target="tpu_custom_call" | custom-call | tf_op jit(solution)/shard_map/klast/pallas_call | solution.py:557
  (193 shorter events, 72.8 us)
Async XLA Ops:
  1.3 20.3 %collective-permute-start.18 = (bf16[1,288,256]{2,1,0:T(8,128)(2,1)S(1)}, bf16[1,288,256]{2,1,0:T(8,128)(2,1)S(1)}, u32[]{:S(2)}, u32[]{:S(2)}) collective-permute-start(bf16[1,288,256]{2,1,0:T(8,128)(2,1)S(1)} %bitcast.35), channel_id=1, source_target_pairs={{0,4},{1,5},{2,6},{3,7},{4,0},{5,1},{6,2},{7,3},{8,12},{9,13},{10,... | collective-permute-start | bytes 442376 | tf_op jit(solution)/shard_map/ppermute | solution.py:388
  19.6 20.3 %collective-permute-start.1 = (bf16[2,72,1152]{2,1,0:T(8,128)(2,1)S(1)}, bf16[2,72,1152]{2,1,0:T(8,128)(2,1)S(1)}, u32[]{:S(2)}, u32[]{:S(2)}) collective-permute-start(bf16[2,72,1152]{2,1,0:T(8,128)(2,1)S(1)} %pad_maximum_fusion.2), channel_id=1, source_target_pairs={{0,2},{1,3},{2,0},{3,1},{4,6},{5,7},{6,4},{7,5},{8,10},{9,11},{10,... | collective-permute-start | bytes 995336 | tf_op jit(solution)/shard_map/ppermute | solution.py:388
  21.7 20.4 %collective-permute-start.19 = (bf16[2,288,256]{2,1,0:T(8,128)(2,1)S(1)}, bf16[2,288,256]{2,1,0:T(8,128)(2,1)S(1)}, u32[]{:S(2)}, u32[]{:S(2)}) collective-permute-start(bf16[2,288,256]{2,1,0:T(8,128)(2,1)S(1)} %pad_maximum_fusion.3), channel_id=1, source_target_pairs={{0,2},{1,3},{2,0},{3,1},{4,6},{5,7},{6,4},{7,5},{8,10},{9,11},{10,... | collective-permute-start | bytes 884744 | tf_op jit(solution)/shard_map/ppermute | solution.py:388
  42.1 34.2 %collective-permute-start.2 = (bf16[4,72,1152]{2,1,0:T(8,128)(2,1)S(1)}, bf16[4,72,1152]{2,1,0:T(8,128)(2,1)S(1)}, u32[]{:S(2)}, u32[]{:S(2)}) collective-permute-start(bf16[4,72,1152]{2,1,0:T(8,128)(2,1)S(1)} %pad_maximum_fusion.refs_11_.refs_15_.refs_10_), channel_id=1, source_target_pairs={{0,1},{1,0},{2,3},{3,2},{4,5},{5,4},{6,7},{7,6},{8,9},{9,8},{10,11... | collective-permute-start | bytes 1990664 | tf_op jit(solution)/shard_map/ppermute | solution.py:388
  43.8 31.0 %collective-permute-start.23 = (bf16[4,288,256]{2,1,0:T(8,128)(2,1)S(1)}, bf16[4,288,256]{2,1,0:T(8,128)(2,1)S(1)}, u32[]{:S(2)}, u32[]{:S(2)}) collective-permute-start(bf16[4,288,256]{2,1,0:T(8,128)(2,1)S(1)} %pad_maximum_fusion.1.refs_19_.refs_23_.refs_18_), channel_id=1, source_target_pairs={{0,8},{8,0},{16,24},{24,16},{1,9},{9,1},{17,25},{25,17},{2,10},{10... | collective-permute-start | bytes 1769480 | tf_op jit(solution)/shard_map/ppermute | solution.py:388
  46.9 30.0 %collective-permute-start.21 = (bf16[4,288,256]{2,1,0:T(8,128)(2,1)S(1)}, bf16[4,288,256]{2,1,0:T(8,128)(2,1)}, u32[]{:S(2)}, u32[]{:S(2)}) collective-permute-start(bf16[4,288,256]{2,1,0:T(8,128)(2,1)S(1)} %pad_maximum_fusion.1.refs_19_.refs_23_.refs_18_), channel_id=1, source_target_pairs={{0,16},{8,24},{16,0},{24,8},{1,17},{9,25},{17,1},{25,9},{2,18},{10... | collective-permute-start | bytes 1769480 | tf_op jit(solution)/shard_map/ppermute | solution.py:388
  49.3 29.5 %collective-permute-start.20 = (bf16[4,288,256]{2,1,0:T(8,128)(2,1)S(1)}, bf16[4,288,256]{2,1,0:T(8,128)(2,1)}, u32[]{:S(2)}, u32[]{:S(2)}) collective-permute-start(bf16[4,288,256]{2,1,0:T(8,128)(2,1)S(1)} %pad_maximum_fusion.1.refs_19_.refs_23_.refs_18_), channel_id=1, source_target_pairs={{0,1},{1,0},{2,3},{3,2},{4,5},{5,4},{6,7},{7,6},{8,9},{9,8},{10,11... | collective-permute-start | bytes 1769480 | tf_op jit(solution)/shard_map/ppermute | solution.py:388
  76.4 42.7 %collective-permute-start.13 = (bf16[4,72,1152]{2,1,0:T(8,128)(2,1)S(1)}, bf16[4,72,1152]{2,1,0:T(8,128)(2,1)}, u32[]{:S(2)}, u32[]{:S(2)}) collective-permute-start(bf16[4,72,1152]{2,1,0:T(8,128)(2,1)S(1)} %collective-permute-done.2.refs_12_.refs_16_.refs_11_), channel_id=1, source_target_pairs={{0,16},{8,24},{16,0},{24,8},{1,17},{9,25},{17,1},{25,9},{2,18},{10... | collective-permute-start | bytes 1990664 | tf_op jit(solution)/shard_map/ppermute | solution.py:388
  78.8 40.3 %collective-permute-start.22 = (bf16[4,288,256]{2,1,0:T(8,128)(2,1)}, bf16[4,288,256]{2,1,0:T(8,128)(2,1)}, u32[]{:S(2)}, u32[]{:S(2)}) collective-permute-start(bf16[4,288,256]{2,1,0:T(8,128)(2,1)} %collective-permute-done.20.refs_20_.refs_24_.refs_19_), channel_id=1, source_target_pairs={{0,16},{8,24},{16,0},{24,8},{1,17},{9,25},{17,1},{25,9},{2,18},{10... | collective-permute-start | bytes 1769480 | tf_op jit(solution)/shard_map/ppermute | solution.py:388
  80.5 39.9 %collective-permute-start.24 = (bf16[4,288,256]{2,1,0:T(8,128)(2,1)}, bf16[4,288,256]{2,1,0:T(8,128)(2,1)}, u32[]{:S(2)}, u32[]{:S(2)}) collective-permute-start(bf16[4,288,256]{2,1,0:T(8,128)(2,1)} %collective-permute-done.20.refs_20_.refs_24_.refs_19_), channel_id=1, source_target_pairs={{0,8},{8,0},{16,24},{24,16},{1,9},{9,1},{17,25},{25,17},{2,10},{10... | collective-permute-start | bytes 1769480 | tf_op jit(solution)/shard_map/ppermute | solution.py:388
  92.8 27.6 %collective-permute-start.15 = (bf16[4,72,1152]{2,1,0:T(8,128)(2,1)S(1)}, bf16[4,72,1152]{2,1,0:T(8,128)(2,1)}, u32[]{:S(2)}, u32[]{:S(2)}) collective-permute-start(bf16[4,72,1152]{2,1,0:T(8,128)(2,1)S(1)} %collective-permute-done.2.refs_12_.refs_16_.refs_11_), channel_id=1, source_target_pairs={{0,8},{8,0},{16,24},{24,16},{1,9},{9,1},{17,25},{25,17},{2,10},{10... | collective-permute-start | bytes 1990664 | tf_op jit(solution)/shard_map/ppermute | solution.py:388
  92.8 27.6 %collective-permute-start.16 = (bf16[4,72,1152]{2,1,0:T(8,128)(2,1)}, bf16[4,72,1152]{2,1,0:T(8,128)(2,1)}, u32[]{:S(2)}, u32[]{:S(2)}) collective-permute-start(bf16[4,72,1152]{2,1,0:T(8,128)(2,1)} %collective-permute-done.12.refs_13_.refs_17_.refs_12_), channel_id=1, source_target_pairs={{0,8},{8,0},{16,24},{24,16},{1,9},{9,1},{17,25},{25,17},{2,10},{10... | collective-permute-start | bytes 1990664 | tf_op jit(solution)/shard_map/ppermute | solution.py:388
  136.0 79.5 %collective-permute-start.34 = (s16[1152,256]{1,0:T(8,128)(2,1)}, s16[1152,256]{1,0:T(8,128)(2,1)S(1)}, u32[]{:S(2)}, u32[]{:S(2)}) collective-permute-start(s16[1152,256]{1,0:T(8,128)(2,1)} %get-tuple-element.59), channel_id=1, source_target_pairs={{0,1},{1,3},{3,2},{2,4},{4,5},{5,7},{7,6},{6,14},{14,15},{15,13},{... | collective-permute-start | bytes 1769480 | tf_op jit(solution)/shard_map/ppermute | solution.py:529
  139.2 19.4 %collective-permute-start.27 = (s16[2,144,256]{2,1,0:T(8,128)(2,1)S(1)}, s16[2,144,256]{2,1,0:T(8,128)(2,1)S(1)}, u32[]{:S(2)}, u32[]{:S(2)}) collective-permute-start(s16[2,144,256]{2,1,0:T(8,128)(2,1)S(1)} %copy-done.38), channel_id=1, source_target_pairs={{0,1},{1,0},{2,3},{3,2},{4,5},{5,4},{6,7},{7,6},{8,9},{9,8},{10,11... | collective-permute-start | bytes 442376 | tf_op jit(solution)/shard_map/ppermute | solution.py:388
  141.1 77.0 %collective-permute-start.35 = (s16[1152,256]{1,0:T(8,128)(2,1)}, s16[1152,256]{1,0:T(8,128)(2,1)S(1)}, u32[]{:S(2)}, u32[]{:S(2)}) collective-permute-start(s16[1152,256]{1,0:T(8,128)(2,1)} %get-tuple-element.60), channel_id=1, source_target_pairs={{1,0},{3,1},{2,3},{4,2},{5,4},{7,5},{6,7},{14,6},{15,14},{13,15},{... | collective-permute-start | bytes 1769480 | tf_op jit(solution)/shard_map/ppermute | solution.py:530
  142.6 18.7 %collective-permute-start.28 = (s16[2,144,256]{2,1,0:T(8,128)(2,1)S(1)}, s16[2,144,256]{2,1,0:T(8,128)(2,1)S(1)}, u32[]{:S(2)}, u32[]{:S(2)}) collective-permute-start(s16[2,144,256]{2,1,0:T(8,128)(2,1)S(1)} %copy-done.37), channel_id=1, source_target_pairs={{0,2},{1,3},{2,0},{3,1},{4,6},{5,7},{6,4},{7,5},{8,10},{9,11},{10,... | collective-permute-start | bytes 442376 | tf_op jit(solution)/shard_map/ppermute | solution.py:388
  161.3 18.6 %collective-permute-start.31 = (s16[2,144,256]{2,1,0:T(8,128)(2,1)}, s16[2,144,256]{2,1,0:T(8,128)(2,1)S(1)}, u32[]{:S(2)}, u32[]{:S(2)}) collective-permute-start(s16[2,144,256]{2,1,0:T(8,128)(2,1)} %get-tuple-element.55), channel_id=1, source_target_pairs={{0,5},{1,4},{2,7},{3,6},{4,1},{5,0},{6,3},{7,2},{8,13},{9,12},{10,... | collective-permute-start | bytes 442376 | tf_op jit(solution)/shard_map/ppermute | solution.py:388
  208.8 27.4 %collective-permute-start.43 = (s16[2,144,256]{2,1,0:T(8,128)(2,1)}, s16[2,144,256]{2,1,0:T(8,128)(2,1)S(1)}, u32[]{:S(2)}, u32[]{:S(2)}) collective-permute-start(s16[2,144,256]{2,1,0:T(8,128)(2,1)} %get-tuple-element.70), channel_id=1, source_target_pairs={{0,1},{1,0},{2,3},{3,2},{4,5},{5,4},{6,7},{7,6},{8,9},{9,8},{10,11... | collective-permute-start | bytes 442376 | tf_op jit(solution)/shard_map/ppermute | solution.py:388
  211.2 27.5 %collective-permute-start.44 = (s16[2,144,256]{2,1,0:T(8,128)(2,1)}, s16[2,144,256]{2,1,0:T(8,128)(2,1)S(1)}, u32[]{:S(2)}, u32[]{:S(2)}) collective-permute-start(s16[2,144,256]{2,1,0:T(8,128)(2,1)} %get-tuple-element.71), channel_id=1, source_target_pairs={{0,2},{1,3},{2,0},{3,1},{4,6},{5,7},{6,4},{7,5},{8,10},{9,11},{10,... | collective-permute-start | bytes 442376 | tf_op jit(solution)/shard_map/ppermute | solution.py:388
  215.1 25.8 %collective-permute-start.45 = (s16[2,144,256]{2,1,0:T(8,128)(2,1)}, s16[2,144,256]{2,1,0:T(8,128)(2,1)S(1)}, u32[]{:S(2)}, u32[]{:S(2)}) collective-permute-start(s16[2,144,256]{2,1,0:T(8,128)(2,1)} %get-tuple-element.72), channel_id=1, source_target_pairs={{0,3},{1,2},{2,1},{3,0},{4,7},{5,6},{6,5},{7,4},{8,11},{9,10},{10,... | collective-permute-start | bytes 442376 | tf_op jit(solution)/shard_map/ppermute | solution.py:388
  215.5 26.2 %collective-permute-start.46 = (s16[2,144,256]{2,1,0:T(8,128)(2,1)}, s16[2,144,256]{2,1,0:T(8,128)(2,1)S(1)}, u32[]{:S(2)}, u32[]{:S(2)}) collective-permute-start(s16[2,144,256]{2,1,0:T(8,128)(2,1)} %get-tuple-element.73), channel_id=1, source_target_pairs={{0,4},{1,5},{2,6},{3,7},{4,0},{5,1},{6,2},{7,3},{8,12},{9,13},{10,... | collective-permute-start | bytes 442376 | tf_op jit(solution)/shard_map/ppermute | solution.py:388
  218.2 23.6 %collective-permute-start.47 = (s16[2,144,256]{2,1,0:T(8,128)(2,1)}, s16[2,144,256]{2,1,0:T(8,128)(2,1)S(1)}, u32[]{:S(2)}, u32[]{:S(2)}) collective-permute-start(s16[2,144,256]{2,1,0:T(8,128)(2,1)} %get-tuple-element.74), channel_id=1, source_target_pairs={{0,5},{1,4},{2,7},{3,6},{4,1},{5,0},{6,3},{7,2},{8,13},{9,12},{10,... | collective-permute-start | bytes 442376 | tf_op jit(solution)/shard_map/ppermute | solution.py:388
  244.9 22.7 %collective-permute-start.39 = (s16[2,144,256]{2,1,0:T(8,128)(2,1)}, s16[2,144,256]{2,1,0:T(8,128)(2,1)S(1)}, u32[]{:S(2)}, u32[]{:S(2)}) collective-permute-start(s16[2,144,256]{2,1,0:T(8,128)(2,1)} %get-tuple-element.65), channel_id=1, source_target_pairs={{0,4},{1,5},{2,6},{3,7},{4,0},{5,1},{6,2},{7,3},{8,12},{9,13},{10,... | collective-permute-start | bytes 442376 | tf_op jit(solution)/shard_map/ppermute | solution.py:388
  250.3 20.9 %collective-permute-start.40 = (s16[2,144,256]{2,1,0:T(8,128)(2,1)}, s16[2,144,256]{2,1,0:T(8,128)(2,1)S(1)}, u32[]{:S(2)}, u32[]{:S(2)}) collective-permute-start(s16[2,144,256]{2,1,0:T(8,128)(2,1)} %get-tuple-element.66), channel_id=1, source_target_pairs={{0,5},{1,4},{2,7},{3,6},{4,1},{5,0},{6,3},{7,2},{8,13},{9,12},{10,... | collective-permute-start | bytes 442376 | tf_op jit(solution)/shard_map/ppermute | solution.py:388
  (67 other events, 1199.9 us)
where the time goes:
time: 281 us; the launch traced here: 278 us
  waiting for transfers between devices  110 us (39%)
  starting transfers between devices  83.5 us (30%)
  Pallas kernels  72.4 us (26%)
  local copies, waits for them, and re-layouts  8.64 us (3%)
  other arithmetic  2.91 us (1%)
    ppermute x46, waiting for transfers between devices, exchange(): return lax.ppermute(array, axis, [(i, i ^ bit) for i in range(count)])  110 us
    ppermute x46, starting transfers between devices, exchange(): return lax.ppermute(array, axis, [(i, i ^ bit) for i in range(count)])  76.1 us
    pallas_call x1, Pallas kernels, body(): pl.pallas_call(lambda *refs: inner_kernel(split, sizes, plan, *refs), in_...  25 us
    pallas_call x1, Pallas kernels, body(): pl.pallas_call(lambda *refs: outer_two_kernel(split, sizes, plan, *refs),...  16.6 us
    pallas_call x1, Pallas kernels, body(): pl.pallas_call(lambda *refs: outer_one_kernel(split, sizes, plan, *refs),...  12.9 us
    pallas_call x1, Pallas kernels, body(): pl.pallas_call(lambda *refs: first_kernel(split, groups, prows, *refs), i...  11.9 us
    pallas_call x1, Pallas kernels, body(): pl.pallas_call(lambda *refs: last_kernel(split, groups, prows, *refs), in...  5.98 us
  transfers between devices with their start and end apart: 50, of which 18 were waited for; matrix products, arithmetic and copies ran while one was open for 3% of the time, Pallas kernels for 19%

commit v1 on v0

--- a/solution.py
+++ b/solution.py
@@ -102,7 +102,7 @@
 
 
 def first_kernel(split, groups, prows, where_ref, numbers_ref, source_ref, low_ref, high_ref, dx_ref, dy_ref, sea_ref, *refs):
-    outs, (spec_ref, shifted_ref, turning_ref, sem) = refs[: len(split) * groups], refs[len(split) * groups :]
+    outs, (spec_ref, turned_ref, sem) = refs[: len(split) * groups], refs[len(split) * groups :]
     channels, cols = low_ref.shape
     rows = groups * prows
     space, device = where_ref[0], where_ref[1]
@@ -122,7 +122,9 @@
         copy(f).wait()
         courant, refract = numbers_ref[0, f], numbers_ref[1, f]
         dx, dy = dx_ref[...] * refract, dy_ref[...] * refract
-        for d in range(DIRS):
+        sea = sea_ref[...].astype(f32)
+
+        def flow(d):
             c = f * DIRS + d
             cosine, sine = math.cos(angles[d]), math.sin(angles[d])
             center = spec_ref[pl.ds(pl.multiple_of(c * rows, 8), rows), :]
@@ -136,8 +138,19 @@
                 behind = jnp.where(lane == cols - 1, 0.0, pltpu.roll(center, cols - 1, 1))
             sx, sy = courant * abs(cosine), courant * abs(sine)
             shifted = center * (1.0 - sx - sy) + beside * sx + behind * sy
-            shifted_ref[c] = shifted
-            turning_ref[c] = (sine * dx - cosine * dy) * shifted
+            return shifted, (sine * dx - cosine * dy) * shifted
+
+        final = flow(DIRS - 1)
+        here = flow(0)
+        before, opening = final[1], here[1]
+        for d in range(DIRS):
+            if d + 1 < DIRS - 1:
+                following = flow(d + 1)
+            else:
+                following = final if d + 1 == DIRS - 1 else (None, opening)
+            value = here[0] - jnp.abs(here[1]) + jnp.maximum(before, 0.0) - jnp.minimum(following[1], 0.0)
+            turned_ref[f * DIRS + d] = value * sea
+            before, here = here[1], following
 
     some = 16 if channels % 16 == 0 else 8
 
@@ -153,15 +166,7 @@
             at = pl.multiple_of(n * some, some)
             for h in range(cols // 128):
                 lanes = pl.ds(h * 128, 128)
-                sea = sea_ref[tall, lanes].astype(f32)
-                tile = []
-                for i in range(some):
-                    c = at + i
-                    d = c % DIRS
-                    before = turning_ref[jnp.where(d == 0, c + DIRS - 1, c - 1), tall, lanes]
-                    after = turning_ref[jnp.where(d == DIRS - 1, c - DIRS + 1, c + 1), tall, lanes]
-                    value = shifted_ref[c, tall, lanes] - jnp.abs(turning_ref[c, tall, lanes])
-                    tile.append((value + jnp.maximum(before, 0.0) - jnp.minimum(after, 0.0)) * sea)
+                tile = [turned_ref[at + i, tall, lanes] for i in range(some)]
                 tile = encode(jnp.swapaxes(jnp.stack(tile), 0, 1))
                 for slot in range(share):
                     for j in range(prows):
@@ -294,35 +299,28 @@
     return list(refs[:count]), refs[count:]
 
 
-def outer_one_kernel(split, sizes, plan, where_ref, numbers_ref, angle_ref, *refs):
-    groups, spaces, _ = sizes
-    codes, refs = take(refs, groups)
-    parts, refs = take(refs, len(plan))
-    (field_ref, *edges), refs = take(refs, 3)
-    net = Net(plan, groups, spaces, where_ref[0], parts, refs)
-    step_one(split[0], codes, field_ref, where_ref[1], net)
-    for edge, n in zip(edges, (0, len(split[0]) - 1)):
-        edge[...] = encode(field_ref[n])
-
-
-def inner_kernel(split, sizes, plan, where_ref, *refs):
+def step_kernel(split, sizes, plan, where_ref, *refs):
     groups, spaces, prows = sizes
     grid, refs = take(refs, 5)
-    (outer_ref,), refs = take(refs, 1)
-    codes, refs = take(refs, groups)
+    codes, refs = take(refs, groups * len(split))
     parts, refs = take(refs, len(plan))
-    (field_ref,), refs = take(refs, 1)
-    outs, refs = take(refs, groups)
+    fields, refs = take(refs, len(split))
+    edges, refs = take(refs, 2)
+    outs, refs = take(refs, groups * (len(split) - 1))
     (moved_ref, coefw), scratch = take(refs, 2)
     space, device = where_ref[0], where_ref[1]
     net = Net(plan, groups, spaces, space, parts, scratch)
-    step_one(split[1], codes, field_ref, device, net)
+    for m, members in enumerate(split):
+        step_one(members, codes[m * groups : (m + 1) * groups], fields[m], device, net)
+    for edge, n in zip(edges, (0, len(split[0]) - 1)):
+        edge[...] = encode(fields[0][n])
 
     def held(j):
-        return (outer_ref, split[0].index(j)) if j in split[0] else (field_ref, split[1].index(j))
-
-    first_row = position_of(device, space, groups) * prows
-    step_two(split[1], held, outs, grid, coefw, moved_ref, first_row, device, net)
+        return (fields[0], split[0].index(j)) if j in split[0] else (fields[1], split[1].index(j))
+
+    if len(split) > 1:
+        first_row = position_of(device, space, groups) * prows
+        step_two(split[1], held, outs, grid, coefw, moved_ref, first_row, device, net)
 
 
 def outer_two_kernel(split, sizes, plan, where_ref, *refs):
@@ -496,7 +494,7 @@
         out_specs=[vmem] * (len(split) * groups),
         out_shape=[shape for own in split for shape in code_shapes(own)],
         scratch_shapes=[pltpu.VMEM((local * rows, cols), f32)]
-        + [pltpu.VMEM((local, rows, cols), f32)] * 2
+        + [pltpu.VMEM((local, rows, cols), f32)]
         + [pltpu.SemaphoreType.DMA((freqs,))],
         compiler_params=params,
         name="kfirst",
@@ -510,16 +508,19 @@
         return jax.ShapeDtypeStruct((len(own), channels, cols), f32)
 
     edge_shape = jax.ShapeDtypeStruct((channels, cols), i16)
-    field, *edge = pl.pallas_call(
-        lambda *refs: outer_one_kernel(split, sizes, plan, *refs),
-        in_specs=[smem, smem, any_spec] + [vmem] * groups + [any_spec] * len(plan),
-        out_specs=[vmem] * 3,
-        out_shape=[field_shape(outer), edge_shape, edge_shape],
-        scratch_shapes=net_scratch,
+    grid = (numbers, angles, depth_dx, depth_dy, land_sea)
+    made = pl.pallas_call(
+        lambda *refs: step_kernel(split, sizes, plan, *refs),
+        in_specs=[smem, smem] + [vmem] * (4 + groups * len(split)) + [any_spec] * len(plan),
+        out_specs=[vmem] * (len(split) + 2 + groups * len(split[1:])),
+        out_shape=[field_shape(own) for own in split]
+        + [edge_shape] * 2
+        + [shape for own in split[1:] for shape in code_shapes(own)],
+        scratch_shapes=step_scratch + net_scratch,
         compiler_params=params,
-        name="kone0",
-    )(place, numbers, angles, *arrived[0], *parts)
-    fields = [field]
+        name="kstep",
+    )(place, *grid, *[code for codes in arrived for code in codes], *parts)
+    fields, edge, sent = made[: len(split)], made[len(split) : len(split) + 2], made[len(split) + 2 :]
 
     chain = []
     for n in range(spaces * groups):
@@ -529,20 +530,7 @@
     low = lax.ppermute(edge[1], ("space", "freq"), chain)
     high = lax.ppermute(edge[0], ("space", "freq"), [(b, a) for a, b in chain])
 
-    grid = (numbers, angles, depth_dx, depth_dy, land_sea)
-    back = []
-    if inner:
-        field, *sent = pl.pallas_call(
-            lambda *refs: inner_kernel(split, sizes, plan, *refs),
-            in_specs=[smem, smem] + [vmem] * (5 + groups) + [any_spec] * len(plan),
-            out_specs=[vmem] * (1 + groups),
-            out_shape=[field_shape(inner)] + code_shapes(inner),
-            scratch_shapes=step_scratch + net_scratch,
-            compiler_params=params,
-            name="kmid",
-        )(place, *grid, fields[0], *arrived[1], *parts)
-        fields.append(field)
-        back = transpose(sent)
+    back = transpose(sent) if inner else []
     sent = pl.pallas_call(
         lambda *refs: outer_two_kernel(split, sizes, plan, *refs),
         in_specs=[smem, smem] + [vmem] * (4 + len(split) + 2) + [any_spec] * len(plan),

time: 281 us -> 267 us (0.950)
  Pallas kernels: 72.4 us -> 65.4 us
  waiting for transfers between devices: 110 us -> 104 us
    ppermute x46, waiting for transfers between devices: 110 us -> 94.7 us  [exchange(): return lax.ppermute(array, axis, [(i, i ^ bit) for i in range(count)])]
    ppermute x1, waiting for transfers between devices: 0.01 us -> 8.78 us  [body(): low = lax.ppermute(edge[1], ('space', 'freq'), chain)]
    pallas_call x2 -> x1, Pallas kernels: 37.9 us -> 32.8 us  [body(): pl.pallas_call(lambda *refs: step_kernel(split, sizes, plan, *refs), in_s...]
  transfers between devices with their start and end apart: 50 -> 50, of which waited for: 18 -> 21; matrix products, arithmetic and copies ran while one was open for 3% -> 3% of each run, Pallas kernels for 19% -> 10%
where the time goes in v1:
time: 267 us; the launch traced here: 263 us
  waiting for transfers between devices  104 us (39%)
  starting transfers between devices  81.6 us (31%)
  Pallas kernels  65.4 us (24%)
  local copies, waits for them, and re-layouts  7.99 us (3%)
  other arithmetic  2.92 us (1%)
    ppermute x46, waiting for transfers between devices, exchange(): return lax.ppermute(array, axis, [(i, i ^ bit) for i in range(count)])  94.7 us
    ppermute x46, starting transfers between devices, exchange(): return lax.ppermute(array, axis, [(i, i ^ bit) for i in range(count)])  75.1 us
    pallas_call x1, Pallas kernels, body(): pl.pallas_call(lambda *refs: step_kernel(split, sizes, plan, *refs), in_s...  32.8 us
    pallas_call x1, Pallas kernels, body(): pl.pallas_call(lambda *refs: outer_two_kernel(split, sizes, plan, *refs),...  16.6 us
    pallas_call x1, Pallas kernels, body(): pl.pallas_call(lambda *refs: first_kernel(split, groups, prows, *refs), i...  9.99 us
    ppermute x1, waiting for transfers between devices, body(): low = lax.ppermute(edge[1], ('space', 'freq'), chain)  8.78 us
    pallas_call x1, Pallas kernels, body(): pl.pallas_call(lambda *refs: last_kernel(split, groups, prows, *refs), in...  5.98 us
  transfers between devices with their start and end apart: 50, of which 21 were waited for; matrix products, arithmetic and copies ran while one was open for 3% of the time, Pallas kernels for 10%

profile of v1, /device:TPU:0, one launch (start us, length us, event | category | flops | bytes accessed | tf_op | source)
XLA Modules:
  0.0 262.8 jit_solution(7124825762818972032)
XLA Ops:
  1.3 4.1 %collective-permute-start.25 = (bf16[1,288,256]{2,1,0:T(8,128)(2,1)S(1)}, bf16[1,288,256]{2,1,0:T(8,128)(2,1)S(1)}, u32[]{:S(2)}, u32[]{:S(2)}) collective-permute-start(bf16[1,288,256]{2,1,0:T(8,128)(2,1)S(1)} %bitcast.35), channel_id=1, source_target_pairs={{0,4},{1,5},{2,6},{3,7},{4,0},{5,1},{6,2},{7,3},{8,12},{9,13},{10,... | collective-permute-start | bytes 442376 | tf_op jit(solution)/shard_map/ppermute | solution.py:386
  12.8 6.8 %collective-permute-done = bf16[1,72,1152]{2,1,0:T(8,128)(2,1)S(1)} collective-permute-done((bf16[1,72,1152]{2,1,0:T(8,128)(2,1)S(1)}, bf16[1,72,1152]{2,1,0:T(8,128)(2,1)S(1)}, u32[]{:S(2)}, u32[]{:S(2)}) %collective-permute-start) | collective-permute-done | bytes 165920 | tf_op jit(solution)/shard_map/ppermute | solution.py:386
  23.0 10.0 %kfirst.1 = (s16[2,144,256]{2,1,0:T(8,128)(2,1)}, s16[2,144,256]{2,1,0:T(8,128)(2,1)}, s16[2,144,256]{2,1,0:T(8,128)(2,1)}, s16[2,144,256]{2,1,0:T(8,128)(2,1)},...) custom-call(s32[2]{0:T(128)} %pad_add_fusion.refs_0_, ...), custom_call_target="tpu_custom_call" | custom-call | tf_op jit(solution)/shard_map/kfirst/pallas_call | solution.py:491
  36.6 3.4 %collective-permute-start.8 = (s16[2,144,256]{2,1,0:T(8,128)(2,1)}, s16[2,144,256]{2,1,0:T(8,128)(2,1)S(1)}, u32[]{:S(2)}, u32[]{:S(2)}) collective-permute-start(s16[2,144,256]{2,1,0:T(8,128)(2,1)} %get-tuple-element.45), channel_id=1, source_target_pairs={{0,4},{1,5},{2,6},{3,7},{4,0},{5,1},{6,2},{7,3},{8,12},{9,13},{10,... | collective-permute-start | bytes 442376 | tf_op jit(solution)/shard_map/ppermute | solution.py:386
  40.6 5.7 %collective-permute-done.6.refs_8_ = s16[2,144,256]{2,1,0:T(8,128)(2,1)S(1)} collective-permute-done((s16[2,144,256]{2,1,0:T(8,128)(2,1)}, s16[2,144,256]{2,1,0:T(8,128)(2,1)S(1)}, u32[]{:S(2)}, u32[]{:S(2)}) %collective-permute-start.6) | collective-permute-done | bytes 147488 | tf_op jit(solution)/shard_map/ppermute | solution.py:386
  46.3 3.1 %collective-permute-done.7.refs_9_ = s16[2,144,256]{2,1,0:T(8,128)(2,1)S(1)} collective-permute-done((s16[2,144,256]{2,1,0:T(8,128)(2,1)}, s16[2,144,256]{2,1,0:T(8,128)(2,1)S(1)}, u32[]{:S(2)}, u32[]{:S(2)}) %collective-permute-start.7) | collective-permute-done | bytes 147488 | tf_op jit(solution)/shard_map/ppermute | solution.py:386
  51.7 3.1 %collective-permute-start.11 = (s16[2,144,256]{2,1,0:T(8,128)(2,1)}, s16[2,144,256]{2,1,0:T(8,128)(2,1)S(1)}, u32[]{:S(2)}, u32[]{:S(2)}) collective-permute-start(s16[2,144,256]{2,1,0:T(8,128)(2,1)} %get-tuple-element.48), channel_id=1, source_target_pairs={{0,7},{1,6},{2,5},{3,4},{4,3},{5,2},{6,1},{7,0},{8,15},{9,14},{10,... | collective-permute-start | bytes 442376 | tf_op jit(solution)/shard_map/ppermute | solution.py:386
  55.7 5.1 %collective-permute-start.13 = (s16[2,144,256]{2,1,0:T(8,128)(2,1)}, s16[2,144,256]{2,1,0:T(8,128)(2,1)S(1)}, u32[]{:S(2)}, u32[]{:S(2)}) collective-permute-start(s16[2,144,256]{2,1,0:T(8,128)(2,1)} %get-tuple-element.51), channel_id=1, source_target_pairs={{0,2},{1,3},{2,0},{3,1},{4,6},{5,7},{6,4},{7,5},{8,10},{9,11},{10,... | collective-permute-start | bytes 442376 | tf_op jit(solution)/shard_map/ppermute | solution.py:386
  66.5 4.4 %collective-permute-start.15 = (s16[2,144,256]{2,1,0:T(8,128)(2,1)}, s16[2,144,256]{2,1,0:T(8,128)(2,1)S(1)}, u32[]{:S(2)}, u32[]{:S(2)}) collective-permute-start(s16[2,144,256]{2,1,0:T(8,128)(2,1)} %get-tuple-element.53), channel_id=1, source_target_pairs={{0,4},{1,5},{2,6},{3,7},{4,0},{5,1},{6,2},{7,3},{8,12},{9,13},{10,... | collective-permute-start | bytes 442376 | tf_op jit(solution)/shard_map/ppermute | solution.py:386
  76.0 8.2 %collective-permute-done.16.refs_19_ = s16[2,144,256]{2,1,0:T(8,128)(2,1)S(1)} collective-permute-done((s16[2,144,256]{2,1,0:T(8,128)(2,1)}, s16[2,144,256]{2,1,0:T(8,128)(2,1)S(1)}, u32[]{:S(2)}, u32[]{:S(2)}) %collective-permute-start.16) | collective-permute-done | bytes 147488 | tf_op jit(solution)/shard_map/ppermute | solution.py:386
  85.6 5.7 %collective-permute-done.17.refs_20_ = s16[2,144,256]{2,1,0:T(8,128)(2,1)S(1)} collective-permute-done((s16[2,144,256]{2,1,0:T(8,128)(2,1)}, s16[2,144,256]{2,1,0:T(8,128)(2,1)S(1)}, u32[]{:S(2)}, u32[]{:S(2)}) %collective-permute-start.17) | collective-permute-done | bytes 147488 | tf_op jit(solution)/shard_map/ppermute | solution.py:386
  91.4 3.1 %collective-permute-start.18 = (s16[2,144,256]{2,1,0:T(8,128)(2,1)}, s16[2,144,256]{2,1,0:T(8,128)(2,1)S(1)}, u32[]{:S(2)}, u32[]{:S(2)}) collective-permute-start(s16[2,144,256]{2,1,0:T(8,128)(2,1)} %get-tuple-element.56), channel_id=1, source_target_pairs={{0,7},{1,6},{2,5},{3,4},{4,3},{5,2},{6,1},{7,0},{8,15},{9,14},{10,... | collective-permute-start | bytes 442376 | tf_op jit(solution)/shard_map/ppermute | solution.py:386
  94.5 5.0 %collective-permute-done.18.refs_21_ = s16[2,144,256]{2,1,0:T(8,128)(2,1)S(1)} collective-permute-done((s16[2,144,256]{2,1,0:T(8,128)(2,1)}, s16[2,144,256]{2,1,0:T(8,128)(2,1)S(1)}, u32[]{:S(2)}, u32[]{:S(2)}) %collective-permute-start.18) | collective-permute-done | bytes 147488 | tf_op jit(solution)/shard_map/ppermute | solution.py:386
  104.7 12.8 %collective-permute-done.19.refs_24_.refs_12_ = bf16[4,72,1152]{2,1,0:T(8,128)(2,1)} collective-permute-done((bf16[4,72,1152]{2,1,0:T(8,128)(2,1)S(1)}, bf16[4,72,1152]{2,1,0:T(8,128)(2,1)}, u32[]{:S(2)}, u32[]{:S(2)}) %collective-permute-start.19) | collective-permute-done | bytes 663584 | tf_op jit(solution)/shard_map/ppermute | solution.py:386
  118.0 25.8 %collective-permute-done.29.refs_33_.refs_21_ = bf16[4,288,256]{2,1,0:T(8,128)(2,1)} collective-permute-done((bf16[4,288,256]{2,1,0:T(8,128)(2,1)}, bf16[4,288,256]{2,1,0:T(8,128)(2,1)}, u32[]{:S(2)}, u32[]{:S(2)}) %collective-permute-start.29) | collective-permute-done | bytes 589856 | tf_op jit(solution)/shard_map/ppermute | solution.py:386
  147.9 32.8 %kstep.1 = (f32[2,1152,256]{2,1,0:T(8,128)}, f32[2,1152,256]{2,1,0:T(8,128)}, s16[1152,256]{1,0:T(8,128)(2,1)}, s16[1152,256]{1,0:T(8,128)(2,1)}, s16[2,144,256]...) custom-call(s32[2]{0:T(128)} %pad_add_fusion.refs_0_, ...), custom_call_target="tpu_custom_call" | custom-call | tf_op jit(solution)/shard_map/kstep/pallas_call | solution.py:512
  189.1 8.8 %collective-permute-done.34.refs_8_ = s16[1152,256]{1,0:T(8,128)(2,1)S(1)} collective-permute-done((s16[1152,256]{1,0:T(8,128)(2,1)}, s16[1152,256]{1,0:T(8,128)(2,1)S(1)}, u32[]{:S(2)}, u32[]{:S(2)}) %collective-permute-start.34) | collective-permute-done | bytes 589856 | tf_op jit(solution)/shard_map/ppermute | solution.py:530
  200.2 3.0 %collective-permute-start.47 = (s16[2,144,256]{2,1,0:T(8,128)(2,1)}, s16[2,144,256]{2,1,0:T(8,128)(2,1)S(1)}, u32[]{:S(2)}, u32[]{:S(2)}) collective-permute-start(s16[2,144,256]{2,1,0:T(8,128)(2,1)} %get-tuple-element.74), channel_id=1, source_target_pairs={{0,5},{1,4},{2,7},{3,6},{4,1},{5,0},{6,3},{7,2},{8,13},{9,12},{10,... | collective-permute-start | bytes 442376 | tf_op jit(solution)/shard_map/ppermute | solution.py:386
  203.2 16.6 %ktwo0.1 = (s16[2,144,256]{2,1,0:T(8,128)(2,1)}, s16[2,144,256]{2,1,0:T(8,128)(2,1)}, s16[2,144,256]{2,1,0:T(8,128)(2,1)}, s16[2,144,256]{2,1,0:T(8,128)(2,1)}, ...) custom-call(s32[2]{0:T(128)} %pad_add_fusion.refs_0_, ...), custom_call_target="tpu_custom_call" | custom-call | tf_op jit(solution)/shard_map/ktwo0/pallas_call | solution.py:534
  219.9 2.9 %collective-permute-start.48 = (s16[2,144,256]{2,1,0:T(8,128)(2,1)S(1)}, s16[2,144,256]{2,1,0:T(8,128)(2,1)S(1)}, u32[]{:S(2)}, u32[]{:S(2)}) collective-permute-start(s16[2,144,256]{2,1,0:T(8,128)(2,1)S(1)} %copy-done.39), channel_id=1, source_target_pairs={{0,6},{1,7},{2,4},{3,5},{4,2},{5,3},{6,0},{7,1},{8,14},{9,15},{10,... | collective-permute-start | bytes 442376 | tf_op jit(solution)/shard_map/ppermute | solution.py:386
  228.1 6.5 %collective-permute-start.39 = (s16[2,144,256]{2,1,0:T(8,128)(2,1)}, s16[2,144,256]{2,1,0:T(8,128)(2,1)S(1)}, u32[]{:S(2)}, u32[]{:S(2)}) collective-permute-start(s16[2,144,256]{2,1,0:T(8,128)(2,1)} %get-tuple-element.65), channel_id=1, source_target_pairs={{0,4},{1,5},{2,6},{3,7},{4,0},{5,1},{6,2},{7,3},{8,12},{9,13},{10,... | collective-permute-start | bytes 442376 | tf_op jit(solution)/shard_map/ppermute | solution.py:386
  234.7 6.4 %collective-permute-start.40 = (s16[2,144,256]{2,1,0:T(8,128)(2,1)}, s16[2,144,256]{2,1,0:T(8,128)(2,1)S(1)}, u32[]{:S(2)}, u32[]{:S(2)}) collective-permute-start(s16[2,144,256]{2,1,0:T(8,128)(2,1)} %get-tuple-element.66), channel_id=1, source_target_pairs={{0,5},{1,4},{2,7},{3,6},{4,1},{5,0},{6,3},{7,2},{8,13},{9,12},{10,... | collective-permute-start | bytes 442376 | tf_op jit(solution)/shard_map/ppermute | solution.py:386
  244.2 9.0 %collective-permute-done.39.refs_5_ = s16[2,144,256]{2,1,0:T(8,128)(2,1)S(1)} collective-permute-done((s16[2,144,256]{2,1,0:T(8,128)(2,1)}, s16[2,144,256]{2,1,0:T(8,128)(2,1)S(1)}, u32[]{:S(2)}, u32[]{:S(2)}) %collective-permute-start.39) | collective-permute-done | bytes 147488 | tf_op jit(solution)/shard_map/ppermute | solution.py:386
  256.8 6.0 %klast.1 = f32[4608,256]{1,0:T(8,128)} custom-call(s32[2]{0:T(128)} %pad_add_fusion.refs_0_, s16[2,144,256]{2,1,0:T(8,128)(2,1)} %get-tuple-element.61.refs_1_, s16[2,144,256]{2,1,0:T(8,128)(2,1)} %copy-done.15, s16[2,144,256]{2,1,0:T(8,128)(2,1)} %copy-done.16, s16[2,144,256]{2,1,0:T(8,128)(2,1)} %copy-done.17, s16[2,144,256]{2,1,0:T(8,128)(2,1)} %copy-done.18, ...), custom_call_target="tpu_custom_call" | custom-call | tf_op jit(solution)/shard_map/klast/pallas_call | solution.py:545
  (190 shorter events, 63.7 us)
Async XLA Ops:
  1.3 35.3 %collective-permute-start.25 = (bf16[1,288,256]{2,1,0:T(8,128)(2,1)S(1)}, bf16[1,288,256]{2,1,0:T(8,128)(2,1)S(1)}, u32[]{:S(2)}, u32[]{:S(2)}) collective-permute-start(bf16[1,288,256]{2,1,0:T(8,128)(2,1)S(1)} %bitcast.35), channel_id=1, source_target_pairs={{0,4},{1,5},{2,6},{3,7},{4,0},{5,1},{6,2},{7,3},{8,12},{9,13},{10,... | collective-permute-start | bytes 442376 | tf_op jit(solution)/shard_map/ppermute | solution.py:386
  19.6 35.2 %collective-permute-start.1 = (bf16[2,72,1152]{2,1,0:T(8,128)(2,1)S(1)}, bf16[2,72,1152]{2,1,0:T(8,128)(2,1)S(1)}, u32[]{:S(2)}, u32[]{:S(2)}) collective-permute-start(bf16[2,72,1152]{2,1,0:T(8,128)(2,1)S(1)} %pad_maximum_fusion.2), channel_id=1, source_target_pairs={{0,2},{1,3},{2,0},{3,1},{4,6},{5,7},{6,4},{7,5},{8,10},{9,11},{10,... | collective-permute-start | bytes 995336 | tf_op jit(solution)/shard_map/ppermute | solution.py:386
  40.0 30.9 %collective-permute-start.26 = (bf16[2,288,256]{2,1,0:T(8,128)(2,1)S(1)}, bf16[2,288,256]{2,1,0:T(8,128)(2,1)S(1)}, u32[]{:S(2)}, u32[]{:S(2)}) collective-permute-start(bf16[2,288,256]{2,1,0:T(8,128)(2,1)S(1)} %pad_maximum_fusion.3), channel_id=1, source_target_pairs={{0,2},{1,3},{2,0},{3,1},{4,6},{5,7},{6,4},{7,5},{8,10},{9,11},{10,... | collective-permute-start | bytes 884744 | tf_op jit(solution)/shard_map/ppermute | solution.py:386
  70.9 30.2 %collective-permute-start.2 = (bf16[4,72,1152]{2,1,0:T(8,128)(2,1)S(1)}, bf16[4,72,1152]{2,1,0:T(8,128)(2,1)S(1)}, u32[]{:S(2)}, u32[]{:S(2)}) collective-permute-start(bf16[4,72,1152]{2,1,0:T(8,128)(2,1)S(1)} %pad_maximum_fusion.refs_22_.refs_10_), channel_id=1, source_target_pairs={{0,1},{1,0},{2,3},{3,2},{4,5},{5,4},{6,7},{7,6},{8,9},{9,8},{10,11... | collective-permute-start | bytes 1990664 | tf_op jit(solution)/shard_map/ppermute | solution.py:386
  71.0 28.6 %collective-permute-start.30 = (bf16[4,288,256]{2,1,0:T(8,128)(2,1)S(1)}, bf16[4,288,256]{2,1,0:T(8,128)(2,1)S(1)}, u32[]{:S(2)}, u32[]{:S(2)}) collective-permute-start(bf16[4,288,256]{2,1,0:T(8,128)(2,1)S(1)} %pad_maximum_fusion.1.refs_30_.refs_18_), channel_id=1, source_target_pairs={{0,8},{8,0},{16,24},{24,16},{1,9},{9,1},{17,25},{25,17},{2,10},{10... | collective-permute-start | bytes 1769480 | tf_op jit(solution)/shard_map/ppermute | solution.py:386
  71.1 30.6 %collective-permute-start.28 = (bf16[4,288,256]{2,1,0:T(8,128)(2,1)S(1)}, bf16[4,288,256]{2,1,0:T(8,128)(2,1)}, u32[]{:S(2)}, u32[]{:S(2)}) collective-permute-start(bf16[4,288,256]{2,1,0:T(8,128)(2,1)S(1)} %pad_maximum_fusion.1.refs_30_.refs_18_), channel_id=1, source_target_pairs={{0,16},{8,24},{16,0},{24,8},{1,17},{9,25},{17,1},{25,9},{2,18},{10... | collective-permute-start | bytes 1769480 | tf_op jit(solution)/shard_map/ppermute | solution.py:386
  73.2 29.6 %collective-permute-start.27 = (bf16[4,288,256]{2,1,0:T(8,128)(2,1)S(1)}, bf16[4,288,256]{2,1,0:T(8,128)(2,1)}, u32[]{:S(2)}, u32[]{:S(2)}) collective-permute-start(bf16[4,288,256]{2,1,0:T(8,128)(2,1)S(1)} %pad_maximum_fusion.1.refs_30_.refs_18_), channel_id=1, source_target_pairs={{0,1},{1,0},{2,3},{3,2},{4,5},{5,4},{6,7},{7,6},{8,9},{9,8},{10,11... | collective-permute-start | bytes 1769480 | tf_op jit(solution)/shard_map/ppermute | solution.py:386
  99.6 18.0 %collective-permute-start.19 = (bf16[4,72,1152]{2,1,0:T(8,128)(2,1)S(1)}, bf16[4,72,1152]{2,1,0:T(8,128)(2,1)}, u32[]{:S(2)}, u32[]{:S(2)}) collective-permute-start(bf16[4,72,1152]{2,1,0:T(8,128)(2,1)S(1)} %pad_maximum_fusion.refs_22_.refs_10_), channel_id=1, source_target_pairs={{0,16},{8,24},{16,0},{24,8},{1,17},{9,25},{17,1},{25,9},{2,18},{10... | collective-permute-start | bytes 1990664 | tf_op jit(solution)/shard_map/ppermute | solution.py:386
  101.1 42.7 %collective-permute-start.20 = (bf16[4,72,1152]{2,1,0:T(8,128)(2,1)S(1)}, bf16[4,72,1152]{2,1,0:T(8,128)(2,1)}, u32[]{:S(2)}, u32[]{:S(2)}) collective-permute-start(bf16[4,72,1152]{2,1,0:T(8,128)(2,1)S(1)} %collective-permute-done.2.refs_23_.refs_11_), channel_id=1, source_target_pairs={{0,16},{8,24},{16,0},{24,8},{1,17},{9,25},{17,1},{25,9},{2,18},{10... | collective-permute-start | bytes 1990664 | tf_op jit(solution)/shard_map/ppermute | solution.py:386
  102.8 41.0 %collective-permute-start.29 = (bf16[4,288,256]{2,1,0:T(8,128)(2,1)}, bf16[4,288,256]{2,1,0:T(8,128)(2,1)}, u32[]{:S(2)}, u32[]{:S(2)}) collective-permute-start(bf16[4,288,256]{2,1,0:T(8,128)(2,1)} %collective-permute-done.27.refs_31_.refs_19_), channel_id=1, source_target_pairs={{0,16},{8,24},{16,0},{24,8},{1,17},{9,25},{17,1},{25,9},{2,18},{10... | collective-permute-start | bytes 1769480 | tf_op jit(solution)/shard_map/ppermute | solution.py:386
  104.6 40.5 %collective-permute-start.31 = (bf16[4,288,256]{2,1,0:T(8,128)(2,1)}, bf16[4,288,256]{2,1,0:T(8,128)(2,1)}, u32[]{:S(2)}, u32[]{:S(2)}) collective-permute-start(bf16[4,288,256]{2,1,0:T(8,128)(2,1)} %collective-permute-done.27.refs_31_.refs_19_), channel_id=1, source_target_pairs={{0,8},{8,0},{16,24},{24,16},{1,9},{9,1},{17,25},{25,17},{2,10},{10... | collective-permute-start | bytes 1769480 | tf_op jit(solution)/shard_map/ppermute | solution.py:386
  117.5 27.6 %collective-permute-start.22 = (bf16[4,72,1152]{2,1,0:T(8,128)(2,1)S(1)}, bf16[4,72,1152]{2,1,0:T(8,128)(2,1)}, u32[]{:S(2)}, u32[]{:S(2)}) collective-permute-start(bf16[4,72,1152]{2,1,0:T(8,128)(2,1)S(1)} %collective-permute-done.2.refs_23_.refs_11_), channel_id=1, source_target_pairs={{0,8},{8,0},{16,24},{24,16},{1,9},{9,1},{17,25},{25,17},{2,10},{10... | collective-permute-start | bytes 1990664 | tf_op jit(solution)/shard_map/ppermute | solution.py:386
  117.5 27.6 %collective-permute-start.23 = (bf16[4,72,1152]{2,1,0:T(8,128)(2,1)}, bf16[4,72,1152]{2,1,0:T(8,128)(2,1)}, u32[]{:S(2)}, u32[]{:S(2)}) collective-permute-start(bf16[4,72,1152]{2,1,0:T(8,128)(2,1)} %collective-permute-done.19.refs_24_.refs_12_), channel_id=1, source_target_pairs={{0,8},{8,0},{16,24},{24,16},{1,9},{9,1},{17,25},{25,17},{2,10},{10... | collective-permute-start | bytes 1990664 | tf_op jit(solution)/shard_map/ppermute | solution.py:386
  180.7 17.2 %collective-permute-start.34 = (s16[1152,256]{1,0:T(8,128)(2,1)}, s16[1152,256]{1,0:T(8,128)(2,1)S(1)}, u32[]{:S(2)}, u32[]{:S(2)}) collective-permute-start(s16[1152,256]{1,0:T(8,128)(2,1)} %get-tuple-element.59), channel_id=1, source_target_pairs={{0,1},{1,3},{3,2},{2,4},{4,5},{5,7},{7,6},{6,14},{14,15},{15,13},{... | collective-permute-start | bytes 1769480 | tf_op jit(solution)/shard_map/ppermute | solution.py:530
  183.1 17.0 %collective-permute-start.35 = (s16[1152,256]{1,0:T(8,128)(2,1)}, s16[1152,256]{1,0:T(8,128)(2,1)S(1)}, u32[]{:S(2)}, u32[]{:S(2)}) collective-permute-start(s16[1152,256]{1,0:T(8,128)(2,1)} %get-tuple-element.60), channel_id=1, source_target_pairs={{1,0},{3,1},{2,3},{4,2},{5,4},{7,5},{6,7},{14,6},{15,14},{13,15},{... | collective-permute-start | bytes 1769480 | tf_op jit(solution)/shard_map/ppermute | solution.py:531
  184.4 35.4 %collective-permute-start.43 = (s16[2,144,256]{2,1,0:T(8,128)(2,1)}, s16[2,144,256]{2,1,0:T(8,128)(2,1)S(1)}, u32[]{:S(2)}, u32[]{:S(2)}) collective-permute-start(s16[2,144,256]{2,1,0:T(8,128)(2,1)} %get-tuple-element.70), channel_id=1, source_target_pairs={{0,1},{1,0},{2,3},{3,2},{4,5},{5,4},{6,7},{7,6},{8,9},{9,8},{10,11... | collective-permute-start | bytes 442376 | tf_op jit(solution)/shard_map/ppermute | solution.py:386
  187.2 35.7 %collective-permute-start.44 = (s16[2,144,256]{2,1,0:T(8,128)(2,1)}, s16[2,144,256]{2,1,0:T(8,128)(2,1)S(1)}, u32[]{:S(2)}, u32[]{:S(2)}) collective-permute-start(s16[2,144,256]{2,1,0:T(8,128)(2,1)} %get-tuple-element.71), channel_id=1, source_target_pairs={{0,2},{1,3},{2,0},{3,1},{4,6},{5,7},{6,4},{7,5},{8,10},{9,11},{10,... | collective-permute-start | bytes 442376 | tf_op jit(solution)/shard_map/ppermute | solution.py:386
  187.8 36.5 %collective-permute-start.45 = (s16[2,144,256]{2,1,0:T(8,128)(2,1)}, s16[2,144,256]{2,1,0:T(8,128)(2,1)S(1)}, u32[]{:S(2)}, u32[]{:S(2)}) collective-permute-start(s16[2,144,256]{2,1,0:T(8,128)(2,1)} %get-tuple-element.72), channel_id=1, source_target_pairs={{0,3},{1,2},{2,1},{3,0},{4,7},{5,6},{6,5},{7,4},{8,11},{9,10},{10,... | collective-permute-start | bytes 442376 | tf_op jit(solution)/shard_map/ppermute | solution.py:386
  197.9 27.4 %collective-permute-start.46 = (s16[2,144,256]{2,1,0:T(8,128)(2,1)}, s16[2,144,256]{2,1,0:T(8,128)(2,1)S(1)}, u32[]{:S(2)}, u32[]{:S(2)}) collective-permute-start(s16[2,144,256]{2,1,0:T(8,128)(2,1)} %get-tuple-element.73), channel_id=1, source_target_pairs={{0,4},{1,5},{2,6},{3,7},{4,0},{5,1},{6,2},{7,3},{8,12},{9,13},{10,... | collective-permute-start | bytes 442376 | tf_op jit(solution)/shard_map/ppermute | solution.py:386
  200.2 26.7 %collective-permute-start.47 = (s16[2,144,256]{2,1,0:T(8,128)(2,1)}, s16[2,144,256]{2,1,0:T(8,128)(2,1)S(1)}, u32[]{:S(2)}, u32[]{:S(2)}) collective-permute-start(s16[2,144,256]{2,1,0:T(8,128)(2,1)} %get-tuple-element.74), channel_id=1, source_target_pairs={{0,5},{1,4},{2,7},{3,6},{4,1},{5,0},{6,3},{7,2},{8,13},{9,12},{10,... | collective-permute-start | bytes 442376 | tf_op jit(solution)/shard_map/ppermute | solution.py:386
  225.3 17.2 %collective-permute-start.37 = (s16[2,144,256]{2,1,0:T(8,128)(2,1)}, s16[2,144,256]{2,1,0:T(8,128)(2,1)S(1)}, u32[]{:S(2)}, u32[]{:S(2)}) collective-permute-start(s16[2,144,256]{2,1,0:T(8,128)(2,1)} %get-tuple-element.63), channel_id=1, source_target_pairs={{0,2},{1,3},{2,0},{3,1},{4,6},{5,7},{6,4},{7,5},{8,10},{9,11},{10,... | collective-permute-start | bytes 442376 | tf_op jit(solution)/shard_map/ppermute | solution.py:386
  226.8 17.3 %collective-permute-start.38 = (s16[2,144,256]{2,1,0:T(8,128)(2,1)}, s16[2,144,256]{2,1,0:T(8,128)(2,1)S(1)}, u32[]{:S(2)}, u32[]{:S(2)}) collective-permute-start(s16[2,144,256]{2,1,0:T(8,128)(2,1)} %get-tuple-element.64), channel_id=1, source_target_pairs={{0,3},{1,2},{2,1},{3,0},{4,7},{5,6},{6,5},{7,4},{8,11},{9,10},{10,... | collective-permute-start | bytes 442376 | tf_op jit(solution)/shard_map/ppermute | solution.py:386
  228.1 25.0 %collective-permute-start.39 = (s16[2,144,256]{2,1,0:T(8,128)(2,1)}, s16[2,144,256]{2,1,0:T(8,128)(2,1)S(1)}, u32[]{:S(2)}, u32[]{:S(2)}) collective-permute-start(s16[2,144,256]{2,1,0:T(8,128)(2,1)} %get-tuple-element.65), channel_id=1, source_target_pairs={{0,4},{1,5},{2,6},{3,7},{4,0},{5,1},{6,2},{7,3},{8,12},{9,13},{10,... | collective-permute-start | bytes 442376 | tf_op jit(solution)/shard_map/ppermute | solution.py:386
  234.7 21.4 %collective-permute-start.40 = (s16[2,144,256]{2,1,0:T(8,128)(2,1)}, s16[2,144,256]{2,1,0:T(8,128)(2,1)S(1)}, u32[]{:S(2)}, u32[]{:S(2)}) collective-permute-start(s16[2,144,256]{2,1,0:T(8,128)(2,1)} %get-tuple-element.66), channel_id=1, source_target_pairs={{0,5},{1,4},{2,7},{3,6},{4,1},{5,0},{6,3},{7,2},{8,13},{9,12},{10,... | collective-permute-start | bytes 442376 | tf_op jit(solution)/shard_map/ppermute | solution.py:386
  (66 other events, 1387.5 us)

commit v2 on v0

--- a/solution.py
+++ b/solution.py
@@ -102,7 +102,7 @@
 
 
 def first_kernel(split, groups, prows, where_ref, numbers_ref, source_ref, low_ref, high_ref, dx_ref, dy_ref, sea_ref, *refs):
-    outs, (spec_ref, shifted_ref, turning_ref, sem) = refs[: len(split) * groups], refs[len(split) * groups :]
+    outs, (spec_ref, turned_ref, sem) = refs[: len(split) * groups], refs[len(split) * groups :]
     channels, cols = low_ref.shape
     rows = groups * prows
     space, device = where_ref[0], where_ref[1]
@@ -122,7 +122,9 @@
         copy(f).wait()
         courant, refract = numbers_ref[0, f], numbers_ref[1, f]
         dx, dy = dx_ref[...] * refract, dy_ref[...] * refract
-        for d in range(DIRS):
+        sea = sea_ref[...].astype(f32)
+
+        def flow(d):
             c = f * DIRS + d
             cosine, sine = math.cos(angles[d]), math.sin(angles[d])
             center = spec_ref[pl.ds(pl.multiple_of(c * rows, 8), rows), :]
@@ -136,8 +138,19 @@
                 behind = jnp.where(lane == cols - 1, 0.0, pltpu.roll(center, cols - 1, 1))
             sx, sy = courant * abs(cosine), courant * abs(sine)
             shifted = center * (1.0 - sx - sy) + beside * sx + behind * sy
-            shifted_ref[c] = shifted
-            turning_ref[c] = (sine * dx - cosine * dy) * shifted
+            return shifted, (sine * dx - cosine * dy) * shifted
+
+        final = flow(DIRS - 1)
+        here = flow(0)
+        before, opening = final[1], here[1]
+        for d in range(DIRS):
+            if d + 1 < DIRS - 1:
+                following = flow(d + 1)
+            else:
+                following = final if d + 1 == DIRS - 1 else (None, opening)
+            value = here[0] - jnp.abs(here[1]) + jnp.maximum(before, 0.0) - jnp.minimum(following[1], 0.0)
+            turned_ref[f * DIRS + d] = value * sea
+            before, here = here[1], following
 
     some = 16 if channels % 16 == 0 else 8
 
@@ -153,15 +166,7 @@
             at = pl.multiple_of(n * some, some)
             for h in range(cols // 128):
                 lanes = pl.ds(h * 128, 128)
-                sea = sea_ref[tall, lanes].astype(f32)
-                tile = []
-                for i in range(some):
-                    c = at + i
-                    d = c % DIRS
-                    before = turning_ref[jnp.where(d == 0, c + DIRS - 1, c - 1), tall, lanes]
-                    after = turning_ref[jnp.where(d == DIRS - 1, c - DIRS + 1, c + 1), tall, lanes]
-                    value = shifted_ref[c, tall, lanes] - jnp.abs(turning_ref[c, tall, lanes])
-                    tile.append((value + jnp.maximum(before, 0.0) - jnp.minimum(after, 0.0)) * sea)
+                tile = [turned_ref[at + i, tall, lanes] for i in range(some)]
                 tile = encode(jnp.swapaxes(jnp.stack(tile), 0, 1))
                 for slot in range(share):
                     for j in range(prows):
@@ -496,7 +501,7 @@
         out_specs=[vmem] * (len(split) * groups),
         out_shape=[shape for own in split for shape in code_shapes(own)],
         scratch_shapes=[pltpu.VMEM((local * rows, cols), f32)]
-        + [pltpu.VMEM((local, rows, cols), f32)] * 2
+        + [pltpu.VMEM((local, rows, cols), f32)]
         + [pltpu.SemaphoreType.DMA((freqs,))],
         compiler_params=params,
         name="kfirst",

time: 281 us -> 279 us (level)
  no operation moved by 1% of the time
where the time goes in v2:
time: 279 us; the launch traced here: 276 us
  waiting for transfers between devices  110 us (39%)
  starting transfers between devices  83.5 us (30%)
  Pallas kernels  70.7 us (25%)
  local copies, waits for them, and re-layouts  8.64 us (3%)
  other arithmetic  2.91 us (1%)
    ppermute x46, waiting for transfers between devices, exchange(): return lax.ppermute(array, axis, [(i, i ^ bit) for i in range(count)])  110 us
    ppermute x46, starting transfers between devices, exchange(): return lax.ppermute(array, axis, [(i, i ^ bit) for i in range(count)])  76.2 us
    pallas_call x1, Pallas kernels, body(): pl.pallas_call(lambda *refs: inner_kernel(split, sizes, plan, *refs), in_...  25.2 us
    pallas_call x1, Pallas kernels, body(): pl.pallas_call(lambda *refs: outer_two_kernel(split, sizes, plan, *refs),...  16.6 us
    pallas_call x1, Pallas kernels, body(): pl.pallas_call(lambda *refs: outer_one_kernel(split, sizes, plan, *refs),...  12.9 us
    pallas_call x1, Pallas kernels, body(): pl.pallas_call(lambda *refs: first_kernel(split, groups, prows, *refs), i...  10 us
    pallas_call x1, Pallas kernels, body(): pl.pallas_call(lambda *refs: last_kernel(split, groups, prows, *refs), in...  5.98 us
  transfers between devices with their start and end apart: 50, of which 18 were waited for; matrix products, arithmetic and copies ran while one was open for 3% of the time, Pallas kernels for 19%

profile of v2, /device:TPU:0, one launch (start us, length us, event | category | flops | bytes accessed | tf_op | source)
XLA Modules:
  0.0 276.2 jit_solution(6804479662162670752)
XLA Ops:
  1.3 4.1 %collective-permute-start.18 = (bf16[1,288,256]{2,1,0:T(8,128)(2,1)S(1)}, bf16[1,288,256]{2,1,0:T(8,128)(2,1)S(1)}, u32[]{:S(2)}, u32[]{:S(2)}) collective-permute-start(bf16[1,288,256]{2,1,0:T(8,128)(2,1)S(1)} %bitcast.35), channel_id=1, source_target_pairs={{0,4},{1,5},{2,6},{3,7},{4,0},{5,1},{6,2},{7,3},{8,12},{9,13},{10,... | collective-permute-start | bytes 442376 | tf_op jit(solution)/shard_map/ppermute | solution.py:393
  12.8 6.8 %collective-permute-done = bf16[1,72,1152]{2,1,0:T(8,128)(2,1)S(1)} collective-permute-done((bf16[1,72,1152]{2,1,0:T(8,128)(2,1)S(1)}, bf16[1,72,1152]{2,1,0:T(8,128)(2,1)S(1)}, u32[]{:S(2)}, u32[]{:S(2)}) %collective-permute-start) | collective-permute-done | bytes 165920 | tf_op jit(solution)/shard_map/ppermute | solution.py:393
  24.4 10.0 %kfirst.1 = (s16[2,144,256]{2,1,0:T(8,128)(2,1)}, s16[2,144,256]{2,1,0:T(8,128)(2,1)}, s16[2,144,256]{2,1,0:T(8,128)(2,1)}, s16[2,144,256]{2,1,0:T(8,128)(2,1)},...) custom-call(s32[2]{0:T(128)} %pad_add_fusion.refs_0_, ...), custom_call_target="tpu_custom_call" | custom-call | tf_op jit(solution)/shard_map/kfirst/pallas_call | solution.py:498
  50.7 6.7 %collective-permute-done.9.refs_8_ = s16[2,144,256]{2,1,0:T(8,128)(2,1)S(1)} collective-permute-done((s16[2,144,256]{2,1,0:T(8,128)(2,1)}, s16[2,144,256]{2,1,0:T(8,128)(2,1)S(1)}, u32[]{:S(2)}, u32[]{:S(2)}) %collective-permute-start.9) | collective-permute-done | bytes 147488 | tf_op jit(solution)/shard_map/ppermute | solution.py:393
  60.4 4.2 %collective-permute-done.10.refs_9_ = s16[2,144,256]{2,1,0:T(8,128)(2,1)S(1)} collective-permute-done((s16[2,144,256]{2,1,0:T(8,128)(2,1)}, s16[2,144,256]{2,1,0:T(8,128)(2,1)S(1)}, u32[]{:S(2)}, u32[]{:S(2)}) %collective-permute-start.10) | collective-permute-done | bytes 147488 | tf_op jit(solution)/shard_map/ppermute | solution.py:393
  64.6 4.3 %collective-permute-start.11 = (s16[2,144,256]{2,1,0:T(8,128)(2,1)}, s16[2,144,256]{2,1,0:T(8,128)(2,1)}, u32[]{:S(2)}, u32[]{:S(2)}) collective-permute-start(s16[2,144,256]{2,1,0:T(8,128)(2,1)} %get-tuple-element.48), channel_id=1, source_target_pairs={{0,7},{1,6},{2,5},{3,4},{4,3},{5,2},{6,1},{7,0},{8,15},{9,14},{10,... | collective-permute-start | bytes 442376 | tf_op jit(solution)/shard_map/ppermute | solution.py:393
  69.0 3.9 %collective-permute-done.11.refs_10_ = s16[2,144,256]{2,1,0:T(8,128)(2,1)} collective-permute-done((s16[2,144,256]{2,1,0:T(8,128)(2,1)}, s16[2,144,256]{2,1,0:T(8,128)(2,1)}, u32[]{:S(2)}, u32[]{:S(2)}) %collective-permute-start.11) | collective-permute-done | bytes 147488 | tf_op jit(solution)/shard_map/ppermute | solution.py:393
  78.6 12.2 %collective-permute-done.12.refs_13_.refs_17_.refs_12_ = bf16[4,72,1152]{2,1,0:T(8,128)(2,1)} collective-permute-done((bf16[4,72,1152]{2,1,0:T(8,128)(2,1)S(1)}, bf16[4,72,1152]{2,1,0:T(8,128)(2,1)}, u32[]{:S(2)}, u32[]{:S(2)}) %collective-permute-start.12) | collective-permute-done | bytes 663584 | tf_op jit(solution)/shard_map/ppermute | solution.py:393
  91.4 25.8 %collective-permute-done.22.refs_22_.refs_26_.refs_21_ = bf16[4,288,256]{2,1,0:T(8,128)(2,1)} collective-permute-done((bf16[4,288,256]{2,1,0:T(8,128)(2,1)}, bf16[4,288,256]{2,1,0:T(8,128)(2,1)}, u32[]{:S(2)}, u32[]{:S(2)}) %collective-permute-start.22) | collective-permute-done | bytes 589856 | tf_op jit(solution)/shard_map/ppermute | solution.py:393
  121.3 12.9 %kone0.1 = (f32[2,1152,256]{2,1,0:T(8,128)}, s16[1152,256]{1,0:T(8,128)(2,1)}, s16[1152,256]{1,0:T(8,128)(2,1)}) custom-call(s32[2]{0:T(128)} %pad_add_fusion.refs_0_, f32[2,32]{1,0:T(2,128)} %concatenate.23.refs_1_, f32[2,72,128]{2,1,0:T(8,128)} %broadcast_in_dim.12.refs_2_, s16[2,144,256]{2,1,0:T(8,128)(2,1)} %get-tuple-element.41.refs_3_, ...), custom_call_target="tpu_custom_call" | custom-call | tf_op jit(solution)/shard_map/kone0/pallas_call | solution.py:518
  134.1 3.1 %collective-permute-start.34 = (s16[1152,256]{1,0:T(8,128)(2,1)}, s16[1152,256]{1,0:T(8,128)(2,1)S(1)}, u32[]{:S(2)}, u32[]{:S(2)}) collective-permute-start(s16[1152,256]{1,0:T(8,128)(2,1)} %get-tuple-element.59), channel_id=1, source_target_pairs={{0,1},{1,3},{3,2},{2,4},{4,5},{5,7},{7,6},{6,14},{14,15},{15,13},{... | collective-permute-start | bytes 1769480 | tf_op jit(solution)/shard_map/ppermute | solution.py:534
  140.7 4.0 %collective-permute-start.28 = (s16[2,144,256]{2,1,0:T(8,128)(2,1)S(1)}, s16[2,144,256]{2,1,0:T(8,128)(2,1)S(1)}, u32[]{:S(2)}, u32[]{:S(2)}) collective-permute-start(s16[2,144,256]{2,1,0:T(8,128)(2,1)S(1)} %copy-done.37), channel_id=1, source_target_pairs={{0,2},{1,3},{2,0},{3,1},{4,6},{5,7},{6,4},{7,5},{8,10},{9,11},{10,... | collective-permute-start | bytes 442376 | tf_op jit(solution)/shard_map/ppermute | solution.py:393
  144.9 11.8 %collective-permute-done.27.refs_8_ = s16[2,144,256]{2,1,0:T(8,128)(2,1)S(1)} collective-permute-done((s16[2,144,256]{2,1,0:T(8,128)(2,1)S(1)}, s16[2,144,256]{2,1,0:T(8,128)(2,1)S(1)}, u32[]{:S(2)}, u32[]{:S(2)}) %collective-permute-start.27) | collective-permute-done | bytes 147488 | tf_op jit(solution)/shard_map/ppermute | solution.py:393
  161.6 11.6 %collective-permute-done.30.refs_11_ = s16[2,144,256]{2,1,0:T(8,128)(2,1)S(1)} collective-permute-done((s16[2,144,256]{2,1,0:T(8,128)(2,1)}, s16[2,144,256]{2,1,0:T(8,128)(2,1)S(1)}, u32[]{:S(2)}, u32[]{:S(2)}) %collective-permute-start.30) | collective-permute-done | bytes 147488 | tf_op jit(solution)/shard_map/ppermute | solution.py:393
  174.4 3.6 %collective-permute-done.31.refs_12_ = s16[2,144,256]{2,1,0:T(8,128)(2,1)S(1)} collective-permute-done((s16[2,144,256]{2,1,0:T(8,128)(2,1)}, s16[2,144,256]{2,1,0:T(8,128)(2,1)S(1)}, u32[]{:S(2)}, u32[]{:S(2)}) %collective-permute-start.31) | collective-permute-done | bytes 147488 | tf_op jit(solution)/shard_map/ppermute | solution.py:393
  178.0 3.3 %collective-permute-done.33.refs_14_ = s16[2,144,256]{2,1,0:T(8,128)(2,1)S(1)} collective-permute-done((s16[2,144,256]{2,1,0:T(8,128)(2,1)}, s16[2,144,256]{2,1,0:T(8,128)(2,1)S(1)}, u32[]{:S(2)}, u32[]{:S(2)}) %collective-permute-start.33) | collective-permute-done | bytes 147488 | tf_op jit(solution)/shard_map/ppermute | solution.py:393
  181.9 25.2 %kmid.1 = (f32[2,1152,256]{2,1,0:T(8,128)}, s16[2,144,256]{2,1,0:T(8,128)(2,1)}, s16[2,144,256]{2,1,0:T(8,128)(2,1)}, s16[2,144,256]{2,1,0:T(8,128)(2,1)}, s16[2...) custom-call(s32[2]{0:T(128)} %pad_add_fusion.refs_0_, ...), custom_call_target="tpu_custom_call" | custom-call | tf_op jit(solution)/shard_map/kmid/pallas_call | solution.py:540
  209.5 3.9 %collective-permute-start.44 = (s16[2,144,256]{2,1,0:T(8,128)(2,1)}, s16[2,144,256]{2,1,0:T(8,128)(2,1)S(1)}, u32[]{:S(2)}, u32[]{:S(2)}) collective-permute-start(s16[2,144,256]{2,1,0:T(8,128)(2,1)} %get-tuple-element.71), channel_id=1, source_target_pairs={{0,2},{1,3},{2,0},{3,1},{4,6},{5,7},{6,4},{7,5},{8,10},{9,11},{10,... | collective-permute-start | bytes 442376 | tf_op jit(solution)/shard_map/ppermute | solution.py:393
  217.9 16.6 %ktwo0.1 = (s16[2,144,256]{2,1,0:T(8,128)(2,1)}, s16[2,144,256]{2,1,0:T(8,128)(2,1)}, s16[2,144,256]{2,1,0:T(8,128)(2,1)}, s16[2,144,256]{2,1,0:T(8,128)(2,1)}, ...) custom-call(s32[2]{0:T(128)} %pad_add_fusion.refs_0_, ...), custom_call_target="tpu_custom_call" | custom-call | tf_op jit(solution)/shard_map/ktwo0/pallas_call | solution.py:551
  243.2 5.4 %collective-permute-start.39 = (s16[2,144,256]{2,1,0:T(8,128)(2,1)}, s16[2,144,256]{2,1,0:T(8,128)(2,1)S(1)}, u32[]{:S(2)}, u32[]{:S(2)}) collective-permute-start(s16[2,144,256]{2,1,0:T(8,128)(2,1)} %get-tuple-element.65), channel_id=1, source_target_pairs={{0,4},{1,5},{2,6},{3,7},{4,0},{5,1},{6,2},{7,3},{8,12},{9,13},{10,... | collective-permute-start | bytes 442376 | tf_op jit(solution)/shard_map/ppermute | solution.py:393
  248.6 5.6 %collective-permute-start.40 = (s16[2,144,256]{2,1,0:T(8,128)(2,1)}, s16[2,144,256]{2,1,0:T(8,128)(2,1)S(1)}, u32[]{:S(2)}, u32[]{:S(2)}) collective-permute-start(s16[2,144,256]{2,1,0:T(8,128)(2,1)} %get-tuple-element.66), channel_id=1, source_target_pairs={{0,5},{1,4},{2,7},{3,6},{4,1},{5,0},{6,3},{7,2},{8,13},{9,12},{10,... | collective-permute-start | bytes 442376 | tf_op jit(solution)/shard_map/ppermute | solution.py:393
  257.9 7.9 %collective-permute-done.39.refs_5_ = s16[2,144,256]{2,1,0:T(8,128)(2,1)S(1)} collective-permute-done((s16[2,144,256]{2,1,0:T(8,128)(2,1)}, s16[2,144,256]{2,1,0:T(8,128)(2,1)S(1)}, u32[]{:S(2)}, u32[]{:S(2)}) %collective-permute-start.39) | collective-permute-done | bytes 147488 | tf_op jit(solution)/shard_map/ppermute | solution.py:393
  265.9 3.6 %collective-permute-done.40.refs_6_ = s16[2,144,256]{2,1,0:T(8,128)(2,1)S(1)} collective-permute-done((s16[2,144,256]{2,1,0:T(8,128)(2,1)}, s16[2,144,256]{2,1,0:T(8,128)(2,1)S(1)}, u32[]{:S(2)}, u32[]{:S(2)}) %collective-permute-start.40) | collective-permute-done | bytes 147488 | tf_op jit(solution)/shard_map/ppermute | solution.py:393
  270.3 6.0 %klast.1 = f32[4608,256]{1,0:T(8,128)} custom-call(s32[2]{0:T(128)} %pad_add_fusion.refs_0_, s16[2,144,256]{2,1,0:T(8,128)(2,1)} %get-tuple-element.61.refs_1_, s16[2,144,256]{2,1,0:T(8,128)(2,1)} %copy-done.15, s16[2,144,256]{2,1,0:T(8,128)(2,1)} %copy-done.16, s16[2,144,256]{2,1,0:T(8,128)(2,1)} %copy-done.17, s16[2,144,256]{2,1,0:T(8,128)(2,1)} %copy-done.18, ...), custom_call_target="tpu_custom_call" | custom-call | tf_op jit(solution)/shard_map/klast/pallas_call | solution.py:562
  (193 shorter events, 72.9 us)
Async XLA Ops:
  1.3 20.3 %collective-permute-start.18 = (bf16[1,288,256]{2,1,0:T(8,128)(2,1)S(1)}, bf16[1,288,256]{2,1,0:T(8,128)(2,1)S(1)}, u32[]{:S(2)}, u32[]{:S(2)}) collective-permute-start(bf16[1,288,256]{2,1,0:T(8,128)(2,1)S(1)} %bitcast.35), channel_id=1, source_target_pairs={{0,4},{1,5},{2,6},{3,7},{4,0},{5,1},{6,2},{7,3},{8,12},{9,13},{10,... | collective-permute-start | bytes 442376 | tf_op jit(solution)/shard_map/ppermute | solution.py:393
  19.6 18.4 %collective-permute-start.1 = (bf16[2,72,1152]{2,1,0:T(8,128)(2,1)S(1)}, bf16[2,72,1152]{2,1,0:T(8,128)(2,1)S(1)}, u32[]{:S(2)}, u32[]{:S(2)}) collective-permute-start(bf16[2,72,1152]{2,1,0:T(8,128)(2,1)S(1)} %pad_maximum_fusion.2), channel_id=1, source_target_pairs={{0,2},{1,3},{2,0},{3,1},{4,6},{5,7},{6,4},{7,5},{8,10},{9,11},{10,... | collective-permute-start | bytes 995336 | tf_op jit(solution)/shard_map/ppermute | solution.py:393
  21.7 18.5 %collective-permute-start.19 = (bf16[2,288,256]{2,1,0:T(8,128)(2,1)S(1)}, bf16[2,288,256]{2,1,0:T(8,128)(2,1)S(1)}, u32[]{:S(2)}, u32[]{:S(2)}) collective-permute-start(bf16[2,288,256]{2,1,0:T(8,128)(2,1)S(1)} %pad_maximum_fusion.3), channel_id=1, source_target_pairs={{0,2},{1,3},{2,0},{3,1},{4,6},{5,7},{6,4},{7,5},{8,10},{9,11},{10,... | collective-permute-start | bytes 884744 | tf_op jit(solution)/shard_map/ppermute | solution.py:393
  40.2 34.2 %collective-permute-start.2 = (bf16[4,72,1152]{2,1,0:T(8,128)(2,1)S(1)}, bf16[4,72,1152]{2,1,0:T(8,128)(2,1)S(1)}, u32[]{:S(2)}, u32[]{:S(2)}) collective-permute-start(bf16[4,72,1152]{2,1,0:T(8,128)(2,1)S(1)} %pad_maximum_fusion.refs_11_.refs_15_.refs_10_), channel_id=1, source_target_pairs={{0,1},{1,0},{2,3},{3,2},{4,5},{5,4},{6,7},{7,6},{8,9},{9,8},{10,11... | collective-permute-start | bytes 1990664 | tf_op jit(solution)/shard_map/ppermute | solution.py:393
  41.9 31.0 %collective-permute-start.23 = (bf16[4,288,256]{2,1,0:T(8,128)(2,1)S(1)}, bf16[4,288,256]{2,1,0:T(8,128)(2,1)S(1)}, u32[]{:S(2)}, u32[]{:S(2)}) collective-permute-start(bf16[4,288,256]{2,1,0:T(8,128)(2,1)S(1)} %pad_maximum_fusion.1.refs_19_.refs_23_.refs_18_), channel_id=1, source_target_pairs={{0,8},{8,0},{16,24},{24,16},{1,9},{9,1},{17,25},{25,17},{2,10},{10... | collective-permute-start | bytes 1769480 | tf_op jit(solution)/shard_map/ppermute | solution.py:393
  45.0 30.0 %collective-permute-start.21 = (bf16[4,288,256]{2,1,0:T(8,128)(2,1)S(1)}, bf16[4,288,256]{2,1,0:T(8,128)(2,1)}, u32[]{:S(2)}, u32[]{:S(2)}) collective-permute-start(bf16[4,288,256]{2,1,0:T(8,128)(2,1)S(1)} %pad_maximum_fusion.1.refs_19_.refs_23_.refs_18_), channel_id=1, source_target_pairs={{0,16},{8,24},{16,0},{24,8},{1,17},{9,25},{17,1},{25,9},{2,18},{10... | collective-permute-start | bytes 1769480 | tf_op jit(solution)/shard_map/ppermute | solution.py:393
  47.3 29.5 %collective-permute-start.20 = (bf16[4,288,256]{2,1,0:T(8,128)(2,1)S(1)}, bf16[4,288,256]{2,1,0:T(8,128)(2,1)}, u32[]{:S(2)}, u32[]{:S(2)}) collective-permute-start(bf16[4,288,256]{2,1,0:T(8,128)(2,1)S(1)} %pad_maximum_fusion.1.refs_19_.refs_23_.refs_18_), channel_id=1, source_target_pairs={{0,1},{1,0},{2,3},{3,2},{4,5},{5,4},{6,7},{7,6},{8,9},{9,8},{10,11... | collective-permute-start | bytes 1769480 | tf_op jit(solution)/shard_map/ppermute | solution.py:393
  74.5 42.7 %collective-permute-start.13 = (bf16[4,72,1152]{2,1,0:T(8,128)(2,1)S(1)}, bf16[4,72,1152]{2,1,0:T(8,128)(2,1)}, u32[]{:S(2)}, u32[]{:S(2)}) collective-permute-start(bf16[4,72,1152]{2,1,0:T(8,128)(2,1)S(1)} %collective-permute-done.2.refs_12_.refs_16_.refs_11_), channel_id=1, source_target_pairs={{0,16},{8,24},{16,0},{24,8},{1,17},{9,25},{17,1},{25,9},{2,18},{10... | collective-permute-start | bytes 1990664 | tf_op jit(solution)/shard_map/ppermute | solution.py:393
  76.9 40.3 %collective-permute-start.22 = (bf16[4,288,256]{2,1,0:T(8,128)(2,1)}, bf16[4,288,256]{2,1,0:T(8,128)(2,1)}, u32[]{:S(2)}, u32[]{:S(2)}) collective-permute-start(bf16[4,288,256]{2,1,0:T(8,128)(2,1)} %collective-permute-done.20.refs_20_.refs_24_.refs_19_), channel_id=1, source_target_pairs={{0,16},{8,24},{16,0},{24,8},{1,17},{9,25},{17,1},{25,9},{2,18},{10... | collective-permute-start | bytes 1769480 | tf_op jit(solution)/shard_map/ppermute | solution.py:393
  78.6 39.9 %collective-permute-start.24 = (bf16[4,288,256]{2,1,0:T(8,128)(2,1)}, bf16[4,288,256]{2,1,0:T(8,128)(2,1)}, u32[]{:S(2)}, u32[]{:S(2)}) collective-permute-start(bf16[4,288,256]{2,1,0:T(8,128)(2,1)} %collective-permute-done.20.refs_20_.refs_24_.refs_19_), channel_id=1, source_target_pairs={{0,8},{8,0},{16,24},{24,16},{1,9},{9,1},{17,25},{25,17},{2,10},{10... | collective-permute-start | bytes 1769480 | tf_op jit(solution)/shard_map/ppermute | solution.py:393
  90.9 27.6 %collective-permute-start.15 = (bf16[4,72,1152]{2,1,0:T(8,128)(2,1)S(1)}, bf16[4,72,1152]{2,1,0:T(8,128)(2,1)}, u32[]{:S(2)}, u32[]{:S(2)}) collective-permute-start(bf16[4,72,1152]{2,1,0:T(8,128)(2,1)S(1)} %collective-permute-done.2.refs_12_.refs_16_.refs_11_), channel_id=1, source_target_pairs={{0,8},{8,0},{16,24},{24,16},{1,9},{9,1},{17,25},{25,17},{2,10},{10... | collective-permute-start | bytes 1990664 | tf_op jit(solution)/shard_map/ppermute | solution.py:393
  90.9 27.6 %collective-permute-start.16 = (bf16[4,72,1152]{2,1,0:T(8,128)(2,1)}, bf16[4,72,1152]{2,1,0:T(8,128)(2,1)}, u32[]{:S(2)}, u32[]{:S(2)}) collective-permute-start(bf16[4,72,1152]{2,1,0:T(8,128)(2,1)} %collective-permute-done.12.refs_13_.refs_17_.refs_12_), channel_id=1, source_target_pairs={{0,8},{8,0},{16,24},{24,16},{1,9},{9,1},{17,25},{25,17},{2,10},{10... | collective-permute-start | bytes 1990664 | tf_op jit(solution)/shard_map/ppermute | solution.py:393
  134.1 79.7 %collective-permute-start.34 = (s16[1152,256]{1,0:T(8,128)(2,1)}, s16[1152,256]{1,0:T(8,128)(2,1)S(1)}, u32[]{:S(2)}, u32[]{:S(2)}) collective-permute-start(s16[1152,256]{1,0:T(8,128)(2,1)} %get-tuple-element.59), channel_id=1, source_target_pairs={{0,1},{1,3},{3,2},{2,4},{4,5},{5,7},{7,6},{6,14},{14,15},{15,13},{... | collective-permute-start | bytes 1769480 | tf_op jit(solution)/shard_map/ppermute | solution.py:534
  137.2 19.4 %collective-permute-start.27 = (s16[2,144,256]{2,1,0:T(8,128)(2,1)S(1)}, s16[2,144,256]{2,1,0:T(8,128)(2,1)S(1)}, u32[]{:S(2)}, u32[]{:S(2)}) collective-permute-start(s16[2,144,256]{2,1,0:T(8,128)(2,1)S(1)} %copy-done.38), channel_id=1, source_target_pairs={{0,1},{1,0},{2,3},{3,2},{4,5},{5,4},{6,7},{7,6},{8,9},{9,8},{10,11... | collective-permute-start | bytes 442376 | tf_op jit(solution)/shard_map/ppermute | solution.py:393
  139.2 77.2 %collective-permute-start.35 = (s16[1152,256]{1,0:T(8,128)(2,1)}, s16[1152,256]{1,0:T(8,128)(2,1)S(1)}, u32[]{:S(2)}, u32[]{:S(2)}) collective-permute-start(s16[1152,256]{1,0:T(8,128)(2,1)} %get-tuple-element.60), channel_id=1, source_target_pairs={{1,0},{3,1},{2,3},{4,2},{5,4},{7,5},{6,7},{14,6},{15,14},{13,15},{... | collective-permute-start | bytes 1769480 | tf_op jit(solution)/shard_map/ppermute | solution.py:535
  140.7 18.7 %collective-permute-start.28 = (s16[2,144,256]{2,1,0:T(8,128)(2,1)S(1)}, s16[2,144,256]{2,1,0:T(8,128)(2,1)S(1)}, u32[]{:S(2)}, u32[]{:S(2)}) collective-permute-start(s16[2,144,256]{2,1,0:T(8,128)(2,1)S(1)} %copy-done.37), channel_id=1, source_target_pairs={{0,2},{1,3},{2,0},{3,1},{4,6},{5,7},{6,4},{7,5},{8,10},{9,11},{10,... | collective-permute-start | bytes 442376 | tf_op jit(solution)/shard_map/ppermute | solution.py:393
  159.4 18.6 %collective-permute-start.31 = (s16[2,144,256]{2,1,0:T(8,128)(2,1)}, s16[2,144,256]{2,1,0:T(8,128)(2,1)S(1)}, u32[]{:S(2)}, u32[]{:S(2)}) collective-permute-start(s16[2,144,256]{2,1,0:T(8,128)(2,1)} %get-tuple-element.55), channel_id=1, source_target_pairs={{0,5},{1,4},{2,7},{3,6},{4,1},{5,0},{6,3},{7,2},{8,13},{9,12},{10,... | collective-permute-start | bytes 442376 | tf_op jit(solution)/shard_map/ppermute | solution.py:393
  207.1 27.4 %collective-permute-start.43 = (s16[2,144,256]{2,1,0:T(8,128)(2,1)}, s16[2,144,256]{2,1,0:T(8,128)(2,1)S(1)}, u32[]{:S(2)}, u32[]{:S(2)}) collective-permute-start(s16[2,144,256]{2,1,0:T(8,128)(2,1)} %get-tuple-element.70), channel_id=1, source_target_pairs={{0,1},{1,0},{2,3},{3,2},{4,5},{5,4},{6,7},{7,6},{8,9},{9,8},{10,11... | collective-permute-start | bytes 442376 | tf_op jit(solution)/shard_map/ppermute | solution.py:393
  209.5 27.5 %collective-permute-start.44 = (s16[2,144,256]{2,1,0:T(8,128)(2,1)}, s16[2,144,256]{2,1,0:T(8,128)(2,1)S(1)}, u32[]{:S(2)}, u32[]{:S(2)}) collective-permute-start(s16[2,144,256]{2,1,0:T(8,128)(2,1)} %get-tuple-element.71), channel_id=1, source_target_pairs={{0,2},{1,3},{2,0},{3,1},{4,6},{5,7},{6,4},{7,5},{8,10},{9,11},{10,... | collective-permute-start | bytes 442376 | tf_op jit(solution)/shard_map/ppermute | solution.py:393
  213.4 25.8 %collective-permute-start.45 = (s16[2,144,256]{2,1,0:T(8,128)(2,1)}, s16[2,144,256]{2,1,0:T(8,128)(2,1)S(1)}, u32[]{:S(2)}, u32[]{:S(2)}) collective-permute-start(s16[2,144,256]{2,1,0:T(8,128)(2,1)} %get-tuple-element.72), channel_id=1, source_target_pairs={{0,3},{1,2},{2,1},{3,0},{4,7},{5,6},{6,5},{7,4},{8,11},{9,10},{10,... | collective-permute-start | bytes 442376 | tf_op jit(solution)/shard_map/ppermute | solution.py:393
  213.9 26.2 %collective-permute-start.46 = (s16[2,144,256]{2,1,0:T(8,128)(2,1)}, s16[2,144,256]{2,1,0:T(8,128)(2,1)S(1)}, u32[]{:S(2)}, u32[]{:S(2)}) collective-permute-start(s16[2,144,256]{2,1,0:T(8,128)(2,1)} %get-tuple-element.73), channel_id=1, source_target_pairs={{0,4},{1,5},{2,6},{3,7},{4,0},{5,1},{6,2},{7,3},{8,12},{9,13},{10,... | collective-permute-start | bytes 442376 | tf_op jit(solution)/shard_map/ppermute | solution.py:393
  216.4 23.6 %collective-permute-start.47 = (s16[2,144,256]{2,1,0:T(8,128)(2,1)}, s16[2,144,256]{2,1,0:T(8,128)(2,1)S(1)}, u32[]{:S(2)}, u32[]{:S(2)}) collective-permute-start(s16[2,144,256]{2,1,0:T(8,128)(2,1)} %get-tuple-element.74), channel_id=1, source_target_pairs={{0,5},{1,4},{2,7},{3,6},{4,1},{5,0},{6,3},{7,2},{8,13},{9,12},{10,... | collective-permute-start | bytes 442376 | tf_op jit(solution)/shard_map/ppermute | solution.py:393
  243.2 22.7 %collective-permute-start.39 = (s16[2,144,256]{2,1,0:T(8,128)(2,1)}, s16[2,144,256]{2,1,0:T(8,128)(2,1)S(1)}, u32[]{:S(2)}, u32[]{:S(2)}) collective-permute-start(s16[2,144,256]{2,1,0:T(8,128)(2,1)} %get-tuple-element.65), channel_id=1, source_target_pairs={{0,4},{1,5},{2,6},{3,7},{4,0},{5,1},{6,2},{7,3},{8,12},{9,13},{10,... | collective-permute-start | bytes 442376 | tf_op jit(solution)/shard_map/ppermute | solution.py:393
  248.6 20.9 %collective-permute-start.40 = (s16[2,144,256]{2,1,0:T(8,128)(2,1)}, s16[2,144,256]{2,1,0:T(8,128)(2,1)S(1)}, u32[]{:S(2)}, u32[]{:S(2)}) collective-permute-start(s16[2,144,256]{2,1,0:T(8,128)(2,1)} %get-tuple-element.66), channel_id=1, source_target_pairs={{0,5},{1,4},{2,7},{3,6},{4,1},{5,0},{6,3},{7,2},{8,13},{9,12},{10,... | collective-permute-start | bytes 442376 | tf_op jit(solution)/shard_map/ppermute | solution.py:393
  (67 other events, 1198.9 us)

commit v3 on v2

--- a/solution.py
+++ b/solution.py
@@ -2,6 +2,7 @@
 
 import jax
 import jax.numpy as jnp
+import numpy as np
 from jax import lax
 from jax.experimental import pallas as pl
 from jax.experimental.pallas import tpu as pltpu
@@ -462,9 +463,9 @@
         found.update({f: raw[n] for n, (f, s) in enumerate(places)})
     numbers = jnp.concatenate([found[f] for f in range(groups)], axis=1)
 
-    angles = (jnp.arange(DIRS, dtype=f32) + 0.5) * (2.0 * math.pi / DIRS)
-    angles = jnp.stack([jnp.cos(angles), jnp.sin(angles)])
-    angles = jnp.broadcast_to(jnp.tile(angles, (1, 2))[:, :, None], (2, BLOCK, 128))
+    angles = (np.arange(BLOCK) % DIRS + 0.5) * (2.0 * math.pi / DIRS)
+    angles = np.stack([np.cos(angles), np.sin(angles)]).astype(np.float32)
+    angles = jnp.asarray(np.ascontiguousarray(np.broadcast_to(angles[:, :, None], (2, BLOCK, 128))))
     place = jnp.stack([space, freq]).astype(i32)
 
     any_spec = pl.BlockSpec(memory_space=pl.ANY)

time: 279 us -> 278 us (level)
  no operation moved by 1% of the time
where the time goes in v3:
time: 278 us; the launch traced here: 276 us
  waiting for transfers between devices  110 us (40%)
  starting transfers between devices  83.5 us (30%)
  Pallas kernels  70.7 us (25%)
  local copies, waits for them, and re-layouts  7.81 us (3%)
  other arithmetic  2.82 us (1%)
    ppermute x46, waiting for transfers between devices, exchange(): return lax.ppermute(array, axis, [(i, i ^ bit) for i in range(count)])  110 us
    ppermute x46, starting transfers between devices, exchange(): return lax.ppermute(array, axis, [(i, i ^ bit) for i in range(count)])  76.2 us
    pallas_call x1, Pallas kernels, body(): pl.pallas_call(lambda *refs: inner_kernel(split, sizes, plan, *refs), in_...  25.2 us
    pallas_call x1, Pallas kernels, body(): pl.pallas_call(lambda *refs: outer_two_kernel(split, sizes, plan, *refs),...  16.6 us
    pallas_call x1, Pallas kernels, body(): pl.pallas_call(lambda *refs: outer_one_kernel(split, sizes, plan, *refs),...  12.9 us
    pallas_call x1, Pallas kernels, body(): pl.pallas_call(lambda *refs: first_kernel(split, groups, prows, *refs), i...  10 us
    pallas_call x1, Pallas kernels, body(): pl.pallas_call(lambda *refs: last_kernel(split, groups, prows, *refs), in...  5.98 us
  transfers between devices with their start and end apart: 50, of which 18 were waited for; matrix products, arithmetic and copies ran while one was open for 3% of the time, Pallas kernels for 19%

profile of v3, /device:TPU:0, one launch (start us, length us, event | category | flops | bytes accessed | tf_op | source)
XLA Modules:
  0.0 275.6 jit_solution(13604297618830506550)
XLA Ops:
  1.3 4.1 %collective-permute-start.18 = (bf16[1,288,256]{2,1,0:T(8,128)(2,1)S(1)}, bf16[1,288,256]{2,1,0:T(8,128)(2,1)S(1)}, u32[]{:S(2)}, u32[]{:S(2)}) collective-permute-start(bf16[1,288,256]{2,1,0:T(8,128)(2,1)S(1)} %bitcast.35), channel_id=1, source_target_pairs={{0,4},{1,5},{2,6},{3,7},{4,0},{5,1},{6,2},{7,3},{8,12},{9,13},{10,... | collective-permute-start | bytes 442376 | tf_op jit(solution)/shard_map/ppermute | solution.py:394
  12.8 6.8 %collective-permute-done = bf16[1,72,1152]{2,1,0:T(8,128)(2,1)S(1)} collective-permute-done((bf16[1,72,1152]{2,1,0:T(8,128)(2,1)S(1)}, bf16[1,72,1152]{2,1,0:T(8,128)(2,1)S(1)}, u32[]{:S(2)}, u32[]{:S(2)}) %collective-permute-start) | collective-permute-done | bytes 165920 | tf_op jit(solution)/shard_map/ppermute | solution.py:394
  24.4 10.0 %kfirst.1 = (s16[2,144,256]{2,1,0:T(8,128)(2,1)}, s16[2,144,256]{2,1,0:T(8,128)(2,1)}, s16[2,144,256]{2,1,0:T(8,128)(2,1)}, s16[2,144,256]{2,1,0:T(8,128)(2,1)},...) custom-call(s32[2]{0:T(128)} %pad_add_fusion.refs_0_, ...), custom_call_target="tpu_custom_call" | custom-call | tf_op jit(solution)/shard_map/kfirst/pallas_call | solution.py:499
  50.7 6.7 %collective-permute-done.9.refs_8_ = s16[2,144,256]{2,1,0:T(8,128)(2,1)S(1)} collective-permute-done((s16[2,144,256]{2,1,0:T(8,128)(2,1)}, s16[2,144,256]{2,1,0:T(8,128)(2,1)S(1)}, u32[]{:S(2)}, u32[]{:S(2)}) %collective-permute-start.9) | collective-permute-done | bytes 147488 | tf_op jit(solution)/shard_map/ppermute | solution.py:394
  60.4 4.2 %collective-permute-done.10.refs_9_ = s16[2,144,256]{2,1,0:T(8,128)(2,1)S(1)} collective-permute-done((s16[2,144,256]{2,1,0:T(8,128)(2,1)}, s16[2,144,256]{2,1,0:T(8,128)(2,1)S(1)}, u32[]{:S(2)}, u32[]{:S(2)}) %collective-permute-start.10) | collective-permute-done | bytes 147488 | tf_op jit(solution)/shard_map/ppermute | solution.py:394
  64.6 4.3 %collective-permute-start.11 = (s16[2,144,256]{2,1,0:T(8,128)(2,1)}, s16[2,144,256]{2,1,0:T(8,128)(2,1)}, u32[]{:S(2)}, u32[]{:S(2)}) collective-permute-start(s16[2,144,256]{2,1,0:T(8,128)(2,1)} %get-tuple-element.48), channel_id=1, source_target_pairs={{0,7},{1,6},{2,5},{3,4},{4,3},{5,2},{6,1},{7,0},{8,15},{9,14},{10,... | collective-permute-start | bytes 442376 | tf_op jit(solution)/shard_map/ppermute | solution.py:394
  68.9 3.9 %collective-permute-done.11.refs_10_ = s16[2,144,256]{2,1,0:T(8,128)(2,1)} collective-permute-done((s16[2,144,256]{2,1,0:T(8,128)(2,1)}, s16[2,144,256]{2,1,0:T(8,128)(2,1)}, u32[]{:S(2)}, u32[]{:S(2)}) %collective-permute-start.11) | collective-permute-done | bytes 147488 | tf_op jit(solution)/shard_map/ppermute | solution.py:394
  78.5 12.4 %collective-permute-done.12.refs_13_.refs_17_.refs_12_ = bf16[4,72,1152]{2,1,0:T(8,128)(2,1)} collective-permute-done((bf16[4,72,1152]{2,1,0:T(8,128)(2,1)S(1)}, bf16[4,72,1152]{2,1,0:T(8,128)(2,1)}, u32[]{:S(2)}, u32[]{:S(2)}) %collective-permute-start.12) | collective-permute-done | bytes 663584 | tf_op jit(solution)/shard_map/ppermute | solution.py:394
  91.3 25.8 %collective-permute-done.22.refs_22_.refs_26_.refs_21_ = bf16[4,288,256]{2,1,0:T(8,128)(2,1)} collective-permute-done((bf16[4,288,256]{2,1,0:T(8,128)(2,1)}, bf16[4,288,256]{2,1,0:T(8,128)(2,1)}, u32[]{:S(2)}, u32[]{:S(2)}) %collective-permute-start.22) | collective-permute-done | bytes 589856 | tf_op jit(solution)/shard_map/ppermute | solution.py:394
  120.5 12.9 %kone0.1 = (f32[2,1152,256]{2,1,0:T(8,128)}, s16[1152,256]{1,0:T(8,128)(2,1)}, s16[1152,256]{1,0:T(8,128)(2,1)}) custom-call(s32[2]{0:T(128)} %pad_add_fusion.refs_0_, f32[2,32]{1,0:T(2,128)} %concatenate.23.refs_1_, f32[2,72,128]{2,1,0:T(8,128)} %constant.24.clone.refs_2_, s16[2,144,256]{2,1,0:T(8,128)(2,1)} %get-tuple-element.41.refs_3_, ...), custom_call_target="tpu_custom_call" | custom-call | tf_op jit(solution)/shard_map/kone0/pallas_call | solution.py:519
  133.4 3.1 %collective-permute-start.34 = (s16[1152,256]{1,0:T(8,128)(2,1)}, s16[1152,256]{1,0:T(8,128)(2,1)S(1)}, u32[]{:S(2)}, u32[]{:S(2)}) collective-permute-start(s16[1152,256]{1,0:T(8,128)(2,1)} %get-tuple-element.59), channel_id=1, source_target_pairs={{0,1},{1,3},{3,2},{2,4},{4,5},{5,7},{7,6},{6,14},{14,15},{15,13},{... | collective-permute-start | bytes 1769480 | tf_op jit(solution)/shard_map/ppermute | solution.py:535
  140.0 4.0 %collective-permute-start.28 = (s16[2,144,256]{2,1,0:T(8,128)(2,1)S(1)}, s16[2,144,256]{2,1,0:T(8,128)(2,1)S(1)}, u32[]{:S(2)}, u32[]{:S(2)}) collective-permute-start(s16[2,144,256]{2,1,0:T(8,128)(2,1)S(1)} %copy-done.37), channel_id=1, source_target_pairs={{0,2},{1,3},{2,0},{3,1},{4,6},{5,7},{6,4},{7,5},{8,10},{9,11},{10,... | collective-permute-start | bytes 442376 | tf_op jit(solution)/shard_map/ppermute | solution.py:394
  144.1 11.8 %collective-permute-done.27.refs_8_ = s16[2,144,256]{2,1,0:T(8,128)(2,1)S(1)} collective-permute-done((s16[2,144,256]{2,1,0:T(8,128)(2,1)S(1)}, s16[2,144,256]{2,1,0:T(8,128)(2,1)S(1)}, u32[]{:S(2)}, u32[]{:S(2)}) %collective-permute-start.27) | collective-permute-done | bytes 147488 | tf_op jit(solution)/shard_map/ppermute | solution.py:394
  160.8 11.6 %collective-permute-done.30.refs_11_ = s16[2,144,256]{2,1,0:T(8,128)(2,1)S(1)} collective-permute-done((s16[2,144,256]{2,1,0:T(8,128)(2,1)}, s16[2,144,256]{2,1,0:T(8,128)(2,1)S(1)}, u32[]{:S(2)}, u32[]{:S(2)}) %collective-permute-start.30) | collective-permute-done | bytes 147488 | tf_op jit(solution)/shard_map/ppermute | solution.py:394
  173.6 3.6 %collective-permute-done.31.refs_12_ = s16[2,144,256]{2,1,0:T(8,128)(2,1)S(1)} collective-permute-done((s16[2,144,256]{2,1,0:T(8,128)(2,1)}, s16[2,144,256]{2,1,0:T(8,128)(2,1)S(1)}, u32[]{:S(2)}, u32[]{:S(2)}) %collective-permute-start.31) | collective-permute-done | bytes 147488 | tf_op jit(solution)/shard_map/ppermute | solution.py:394
  177.2 3.3 %collective-permute-done.33.refs_14_ = s16[2,144,256]{2,1,0:T(8,128)(2,1)S(1)} collective-permute-done((s16[2,144,256]{2,1,0:T(8,128)(2,1)}, s16[2,144,256]{2,1,0:T(8,128)(2,1)S(1)}, u32[]{:S(2)}, u32[]{:S(2)}) %collective-permute-start.33) | collective-permute-done | bytes 147488 | tf_op jit(solution)/shard_map/ppermute | solution.py:394
  181.2 25.2 %kmid.1 = (f32[2,1152,256]{2,1,0:T(8,128)}, s16[2,144,256]{2,1,0:T(8,128)(2,1)}, s16[2,144,256]{2,1,0:T(8,128)(2,1)}, s16[2,144,256]{2,1,0:T(8,128)(2,1)}, s16[2...) custom-call(s32[2]{0:T(128)} %pad_add_fusion.refs_0_, ...), custom_call_target="tpu_custom_call" | custom-call | tf_op jit(solution)/shard_map/kmid/pallas_call | solution.py:541
  208.7 3.9 %collective-permute-start.44 = (s16[2,144,256]{2,1,0:T(8,128)(2,1)}, s16[2,144,256]{2,1,0:T(8,128)(2,1)S(1)}, u32[]{:S(2)}, u32[]{:S(2)}) collective-permute-start(s16[2,144,256]{2,1,0:T(8,128)(2,1)} %get-tuple-element.71), channel_id=1, source_target_pairs={{0,2},{1,3},{2,0},{3,1},{4,6},{5,7},{6,4},{7,5},{8,10},{9,11},{10,... | collective-permute-start | bytes 442376 | tf_op jit(solution)/shard_map/ppermute | solution.py:394
  217.2 16.6 %ktwo0.1 = (s16[2,144,256]{2,1,0:T(8,128)(2,1)}, s16[2,144,256]{2,1,0:T(8,128)(2,1)}, s16[2,144,256]{2,1,0:T(8,128)(2,1)}, s16[2,144,256]{2,1,0:T(8,128)(2,1)}, ...) custom-call(s32[2]{0:T(128)} %pad_add_fusion.refs_0_, ...), custom_call_target="tpu_custom_call" | custom-call | tf_op jit(solution)/shard_map/ktwo0/pallas_call | solution.py:552
  242.5 5.4 %collective-permute-start.39 = (s16[2,144,256]{2,1,0:T(8,128)(2,1)}, s16[2,144,256]{2,1,0:T(8,128)(2,1)S(1)}, u32[]{:S(2)}, u32[]{:S(2)}) collective-permute-start(s16[2,144,256]{2,1,0:T(8,128)(2,1)} %get-tuple-element.65), channel_id=1, source_target_pairs={{0,4},{1,5},{2,6},{3,7},{4,0},{5,1},{6,2},{7,3},{8,12},{9,13},{10,... | collective-permute-start | bytes 442376 | tf_op jit(solution)/shard_map/ppermute | solution.py:394
  247.9 5.6 %collective-permute-start.40 = (s16[2,144,256]{2,1,0:T(8,128)(2,1)}, s16[2,144,256]{2,1,0:T(8,128)(2,1)S(1)}, u32[]{:S(2)}, u32[]{:S(2)}) collective-permute-start(s16[2,144,256]{2,1,0:T(8,128)(2,1)} %get-tuple-element.66), channel_id=1, source_target_pairs={{0,5},{1,4},{2,7},{3,6},{4,1},{5,0},{6,3},{7,2},{8,13},{9,12},{10,... | collective-permute-start | bytes 442376 | tf_op jit(solution)/shard_map/ppermute | solution.py:394
  257.2 8.0 %collective-permute-done.39.refs_5_ = s16[2,144,256]{2,1,0:T(8,128)(2,1)S(1)} collective-permute-done((s16[2,144,256]{2,1,0:T(8,128)(2,1)}, s16[2,144,256]{2,1,0:T(8,128)(2,1)S(1)}, u32[]{:S(2)}, u32[]{:S(2)}) %collective-permute-start.39) | collective-permute-done | bytes 147488 | tf_op jit(solution)/shard_map/ppermute | solution.py:394
  265.2 3.6 %collective-permute-done.40.refs_6_ = s16[2,144,256]{2,1,0:T(8,128)(2,1)S(1)} collective-permute-done((s16[2,144,256]{2,1,0:T(8,128)(2,1)}, s16[2,144,256]{2,1,0:T(8,128)(2,1)S(1)}, u32[]{:S(2)}, u32[]{:S(2)}) %collective-permute-start.40) | collective-permute-done | bytes 147488 | tf_op jit(solution)/shard_map/ppermute | solution.py:394
  269.6 6.0 %klast.1 = f32[4608,256]{1,0:T(8,128)} custom-call(s32[2]{0:T(128)} %pad_add_fusion.refs_0_, s16[2,144,256]{2,1,0:T(8,128)(2,1)} %get-tuple-element.61.refs_1_, s16[2,144,256]{2,1,0:T(8,128)(2,1)} %copy-done.15, s16[2,144,256]{2,1,0:T(8,128)(2,1)} %copy-done.16, s16[2,144,256]{2,1,0:T(8,128)(2,1)} %copy-done.17, s16[2,144,256]{2,1,0:T(8,128)(2,1)} %copy-done.18, ...), custom_call_target="tpu_custom_call" | custom-call | tf_op jit(solution)/shard_map/klast/pallas_call | solution.py:563
  (188 shorter events, 72.0 us)
Async XLA Ops:
  1.3 20.3 %collective-permute-start.18 = (bf16[1,288,256]{2,1,0:T(8,128)(2,1)S(1)}, bf16[1,288,256]{2,1,0:T(8,128)(2,1)S(1)}, u32[]{:S(2)}, u32[]{:S(2)}) collective-permute-start(bf16[1,288,256]{2,1,0:T(8,128)(2,1)S(1)} %bitcast.35), channel_id=1, source_target_pairs={{0,4},{1,5},{2,6},{3,7},{4,0},{5,1},{6,2},{7,3},{8,12},{9,13},{10,... | collective-permute-start | bytes 442376 | tf_op jit(solution)/shard_map/ppermute | solution.py:394
  19.6 18.3 %collective-permute-start.1 = (bf16[2,72,1152]{2,1,0:T(8,128)(2,1)S(1)}, bf16[2,72,1152]{2,1,0:T(8,128)(2,1)S(1)}, u32[]{:S(2)}, u32[]{:S(2)}) collective-permute-start(bf16[2,72,1152]{2,1,0:T(8,128)(2,1)S(1)} %pad_maximum_fusion.2), channel_id=1, source_target_pairs={{0,2},{1,3},{2,0},{3,1},{4,6},{5,7},{6,4},{7,5},{8,10},{9,11},{10,... | collective-permute-start | bytes 995336 | tf_op jit(solution)/shard_map/ppermute | solution.py:394
  21.7 18.5 %collective-permute-start.19 = (bf16[2,288,256]{2,1,0:T(8,128)(2,1)S(1)}, bf16[2,288,256]{2,1,0:T(8,128)(2,1)S(1)}, u32[]{:S(2)}, u32[]{:S(2)}) collective-permute-start(bf16[2,288,256]{2,1,0:T(8,128)(2,1)S(1)} %pad_maximum_fusion.3), channel_id=1, source_target_pairs={{0,2},{1,3},{2,0},{3,1},{4,6},{5,7},{6,4},{7,5},{8,10},{9,11},{10,... | collective-permute-start | bytes 884744 | tf_op jit(solution)/shard_map/ppermute | solution.py:394
  40.2 34.2 %collective-permute-start.2 = (bf16[4,72,1152]{2,1,0:T(8,128)(2,1)S(1)}, bf16[4,72,1152]{2,1,0:T(8,128)(2,1)S(1)}, u32[]{:S(2)}, u32[]{:S(2)}) collective-permute-start(bf16[4,72,1152]{2,1,0:T(8,128)(2,1)S(1)} %pad_maximum_fusion.refs_11_.refs_15_.refs_10_), channel_id=1, source_target_pairs={{0,1},{1,0},{2,3},{3,2},{4,5},{5,4},{6,7},{7,6},{8,9},{9,8},{10,11... | collective-permute-start | bytes 1990664 | tf_op jit(solution)/shard_map/ppermute | solution.py:394
  41.8 31.0 %collective-permute-start.23 = (bf16[4,288,256]{2,1,0:T(8,128)(2,1)S(1)}, bf16[4,288,256]{2,1,0:T(8,128)(2,1)S(1)}, u32[]{:S(2)}, u32[]{:S(2)}) collective-permute-start(bf16[4,288,256]{2,1,0:T(8,128)(2,1)S(1)} %pad_maximum_fusion.1.refs_19_.refs_23_.refs_18_), channel_id=1, source_target_pairs={{0,8},{8,0},{16,24},{24,16},{1,9},{9,1},{17,25},{25,17},{2,10},{10... | collective-permute-start | bytes 1769480 | tf_op jit(solution)/shard_map/ppermute | solution.py:394
  44.9 30.0 %collective-permute-start.21 = (bf16[4,288,256]{2,1,0:T(8,128)(2,1)S(1)}, bf16[4,288,256]{2,1,0:T(8,128)(2,1)}, u32[]{:S(2)}, u32[]{:S(2)}) collective-permute-start(bf16[4,288,256]{2,1,0:T(8,128)(2,1)S(1)} %pad_maximum_fusion.1.refs_19_.refs_23_.refs_18_), channel_id=1, source_target_pairs={{0,16},{8,24},{16,0},{24,8},{1,17},{9,25},{17,1},{25,9},{2,18},{10... | collective-permute-start | bytes 1769480 | tf_op jit(solution)/shard_map/ppermute | solution.py:394
  47.3 29.5 %collective-permute-start.20 = (bf16[4,288,256]{2,1,0:T(8,128)(2,1)S(1)}, bf16[4,288,256]{2,1,0:T(8,128)(2,1)}, u32[]{:S(2)}, u32[]{:S(2)}) collective-permute-start(bf16[4,288,256]{2,1,0:T(8,128)(2,1)S(1)} %pad_maximum_fusion.1.refs_19_.refs_23_.refs_18_), channel_id=1, source_target_pairs={{0,1},{1,0},{2,3},{3,2},{4,5},{5,4},{6,7},{7,6},{8,9},{9,8},{10,11... | collective-permute-start | bytes 1769480 | tf_op jit(solution)/shard_map/ppermute | solution.py:394
  74.4 42.7 %collective-permute-start.13 = (bf16[4,72,1152]{2,1,0:T(8,128)(2,1)S(1)}, bf16[4,72,1152]{2,1,0:T(8,128)(2,1)}, u32[]{:S(2)}, u32[]{:S(2)}) collective-permute-start(bf16[4,72,1152]{2,1,0:T(8,128)(2,1)S(1)} %collective-permute-done.2.refs_12_.refs_16_.refs_11_), channel_id=1, source_target_pairs={{0,16},{8,24},{16,0},{24,8},{1,17},{9,25},{17,1},{25,9},{2,18},{10... | collective-permute-start | bytes 1990664 | tf_op jit(solution)/shard_map/ppermute | solution.py:394
  76.8 40.3 %collective-permute-start.22 = (bf16[4,288,256]{2,1,0:T(8,128)(2,1)}, bf16[4,288,256]{2,1,0:T(8,128)(2,1)}, u32[]{:S(2)}, u32[]{:S(2)}) collective-permute-start(bf16[4,288,256]{2,1,0:T(8,128)(2,1)} %collective-permute-done.20.refs_20_.refs_24_.refs_19_), channel_id=1, source_target_pairs={{0,16},{8,24},{16,0},{24,8},{1,17},{9,25},{17,1},{25,9},{2,18},{10... | collective-permute-start | bytes 1769480 | tf_op jit(solution)/shard_map/ppermute | solution.py:394
  78.4 40.0 %collective-permute-start.24 = (bf16[4,288,256]{2,1,0:T(8,128)(2,1)}, bf16[4,288,256]{2,1,0:T(8,128)(2,1)}, u32[]{:S(2)}, u32[]{:S(2)}) collective-permute-start(bf16[4,288,256]{2,1,0:T(8,128)(2,1)} %collective-permute-done.20.refs_20_.refs_24_.refs_19_), channel_id=1, source_target_pairs={{0,8},{8,0},{16,24},{24,16},{1,9},{9,1},{17,25},{25,17},{2,10},{10... | collective-permute-start | bytes 1769480 | tf_op jit(solution)/shard_map/ppermute | solution.py:394
  90.8 27.6 %collective-permute-start.15 = (bf16[4,72,1152]{2,1,0:T(8,128)(2,1)S(1)}, bf16[4,72,1152]{2,1,0:T(8,128)(2,1)}, u32[]{:S(2)}, u32[]{:S(2)}) collective-permute-start(bf16[4,72,1152]{2,1,0:T(8,128)(2,1)S(1)} %collective-permute-done.2.refs_12_.refs_16_.refs_11_), channel_id=1, source_target_pairs={{0,8},{8,0},{16,24},{24,16},{1,9},{9,1},{17,25},{25,17},{2,10},{10... | collective-permute-start | bytes 1990664 | tf_op jit(solution)/shard_map/ppermute | solution.py:394
  90.8 27.6 %collective-permute-start.16 = (bf16[4,72,1152]{2,1,0:T(8,128)(2,1)}, bf16[4,72,1152]{2,1,0:T(8,128)(2,1)}, u32[]{:S(2)}, u32[]{:S(2)}) collective-permute-start(bf16[4,72,1152]{2,1,0:T(8,128)(2,1)} %collective-permute-done.12.refs_13_.refs_17_.refs_12_), channel_id=1, source_target_pairs={{0,8},{8,0},{16,24},{24,16},{1,9},{9,1},{17,25},{25,17},{2,10},{10... | collective-permute-start | bytes 1990664 | tf_op jit(solution)/shard_map/ppermute | solution.py:394
  133.4 79.7 %collective-permute-start.34 = (s16[1152,256]{1,0:T(8,128)(2,1)}, s16[1152,256]{1,0:T(8,128)(2,1)S(1)}, u32[]{:S(2)}, u32[]{:S(2)}) collective-permute-start(s16[1152,256]{1,0:T(8,128)(2,1)} %get-tuple-element.59), channel_id=1, source_target_pairs={{0,1},{1,3},{3,2},{2,4},{4,5},{5,7},{7,6},{6,14},{14,15},{15,13},{... | collective-permute-start | bytes 1769480 | tf_op jit(solution)/shard_map/ppermute | solution.py:535
  136.5 19.4 %collective-permute-start.27 = (s16[2,144,256]{2,1,0:T(8,128)(2,1)S(1)}, s16[2,144,256]{2,1,0:T(8,128)(2,1)S(1)}, u32[]{:S(2)}, u32[]{:S(2)}) collective-permute-start(s16[2,144,256]{2,1,0:T(8,128)(2,1)S(1)} %copy-done.38), channel_id=1, source_target_pairs={{0,1},{1,0},{2,3},{3,2},{4,5},{5,4},{6,7},{7,6},{8,9},{9,8},{10,11... | collective-permute-start | bytes 442376 | tf_op jit(solution)/shard_map/ppermute | solution.py:394
  138.5 77.2 %collective-permute-start.35 = (s16[1152,256]{1,0:T(8,128)(2,1)}, s16[1152,256]{1,0:T(8,128)(2,1)S(1)}, u32[]{:S(2)}, u32[]{:S(2)}) collective-permute-start(s16[1152,256]{1,0:T(8,128)(2,1)} %get-tuple-element.60), channel_id=1, source_target_pairs={{1,0},{3,1},{2,3},{4,2},{5,4},{7,5},{6,7},{14,6},{15,14},{13,15},{... | collective-permute-start | bytes 1769480 | tf_op jit(solution)/shard_map/ppermute | solution.py:536
  140.0 18.7 %collective-permute-start.28 = (s16[2,144,256]{2,1,0:T(8,128)(2,1)S(1)}, s16[2,144,256]{2,1,0:T(8,128)(2,1)S(1)}, u32[]{:S(2)}, u32[]{:S(2)}) collective-permute-start(s16[2,144,256]{2,1,0:T(8,128)(2,1)S(1)} %copy-done.37), channel_id=1, source_target_pairs={{0,2},{1,3},{2,0},{3,1},{4,6},{5,7},{6,4},{7,5},{8,10},{9,11},{10,... | collective-permute-start | bytes 442376 | tf_op jit(solution)/shard_map/ppermute | solution.py:394
  158.6 18.6 %collective-permute-start.31 = (s16[2,144,256]{2,1,0:T(8,128)(2,1)}, s16[2,144,256]{2,1,0:T(8,128)(2,1)S(1)}, u32[]{:S(2)}, u32[]{:S(2)}) collective-permute-start(s16[2,144,256]{2,1,0:T(8,128)(2,1)} %get-tuple-element.55), channel_id=1, source_target_pairs={{0,5},{1,4},{2,7},{3,6},{4,1},{5,0},{6,3},{7,2},{8,13},{9,12},{10,... | collective-permute-start | bytes 442376 | tf_op jit(solution)/shard_map/ppermute | solution.py:394
  206.4 27.5 %collective-permute-start.43 = (s16[2,144,256]{2,1,0:T(8,128)(2,1)}, s16[2,144,256]{2,1,0:T(8,128)(2,1)S(1)}, u32[]{:S(2)}, u32[]{:S(2)}) collective-permute-start(s16[2,144,256]{2,1,0:T(8,128)(2,1)} %get-tuple-element.70), channel_id=1, source_target_pairs={{0,1},{1,0},{2,3},{3,2},{4,5},{5,4},{6,7},{7,6},{8,9},{9,8},{10,11... | collective-permute-start | bytes 442376 | tf_op jit(solution)/shard_map/ppermute | solution.py:394
  208.7 27.5 %collective-permute-start.44 = (s16[2,144,256]{2,1,0:T(8,128)(2,1)}, s16[2,144,256]{2,1,0:T(8,128)(2,1)S(1)}, u32[]{:S(2)}, u32[]{:S(2)}) collective-permute-start(s16[2,144,256]{2,1,0:T(8,128)(2,1)} %get-tuple-element.71), channel_id=1, source_target_pairs={{0,2},{1,3},{2,0},{3,1},{4,6},{5,7},{6,4},{7,5},{8,10},{9,11},{10,... | collective-permute-start | bytes 442376 | tf_op jit(solution)/shard_map/ppermute | solution.py:394
  212.7 25.9 %collective-permute-start.45 = (s16[2,144,256]{2,1,0:T(8,128)(2,1)}, s16[2,144,256]{2,1,0:T(8,128)(2,1)S(1)}, u32[]{:S(2)}, u32[]{:S(2)}) collective-permute-start(s16[2,144,256]{2,1,0:T(8,128)(2,1)} %get-tuple-element.72), channel_id=1, source_target_pairs={{0,3},{1,2},{2,1},{3,0},{4,7},{5,6},{6,5},{7,4},{8,11},{9,10},{10,... | collective-permute-start | bytes 442376 | tf_op jit(solution)/shard_map/ppermute | solution.py:394
  213.1 26.2 %collective-permute-start.46 = (s16[2,144,256]{2,1,0:T(8,128)(2,1)}, s16[2,144,256]{2,1,0:T(8,128)(2,1)S(1)}, u32[]{:S(2)}, u32[]{:S(2)}) collective-permute-start(s16[2,144,256]{2,1,0:T(8,128)(2,1)} %get-tuple-element.73), channel_id=1, source_target_pairs={{0,4},{1,5},{2,6},{3,7},{4,0},{5,1},{6,2},{7,3},{8,12},{9,13},{10,... | collective-permute-start | bytes 442376 | tf_op jit(solution)/shard_map/ppermute | solution.py:394
  215.7 23.6 %collective-permute-start.47 = (s16[2,144,256]{2,1,0:T(8,128)(2,1)}, s16[2,144,256]{2,1,0:T(8,128)(2,1)S(1)}, u32[]{:S(2)}, u32[]{:S(2)}) collective-permute-start(s16[2,144,256]{2,1,0:T(8,128)(2,1)} %get-tuple-element.74), channel_id=1, source_target_pairs={{0,5},{1,4},{2,7},{3,6},{4,1},{5,0},{6,3},{7,2},{8,13},{9,12},{10,... | collective-permute-start | bytes 442376 | tf_op jit(solution)/shard_map/ppermute | solution.py:394
  242.5 22.7 %collective-permute-start.39 = (s16[2,144,256]{2,1,0:T(8,128)(2,1)}, s16[2,144,256]{2,1,0:T(8,128)(2,1)S(1)}, u32[]{:S(2)}, u32[]{:S(2)}) collective-permute-start(s16[2,144,256]{2,1,0:T(8,128)(2,1)} %get-tuple-element.65), channel_id=1, source_target_pairs={{0,4},{1,5},{2,6},{3,7},{4,0},{5,1},{6,2},{7,3},{8,12},{9,13},{10,... | collective-permute-start | bytes 442376 | tf_op jit(solution)/shard_map/ppermute | solution.py:394
  247.9 20.9 %collective-permute-start.40 = (s16[2,144,256]{2,1,0:T(8,128)(2,1)}, s16[2,144,256]{2,1,0:T(8,128)(2,1)S(1)}, u32[]{:S(2)}, u32[]{:S(2)}) collective-permute-start(s16[2,144,256]{2,1,0:T(8,128)(2,1)} %get-tuple-element.66), channel_id=1, source_target_pairs={{0,5},{1,4},{2,7},{3,6},{4,1},{5,0},{6,3},{7,2},{8,13},{9,12},{10,... | collective-permute-start | bytes 442376 | tf_op jit(solution)/shard_map/ppermute | solution.py:394
  (67 other events, 1195.4 us)

commit v4 on v3

--- a/solution.py
+++ b/solution.py
@@ -356,12 +356,12 @@
 
 
 def last_kernel(split, groups, prows, where_ref, *refs):
-    codes, out_ref = refs[:-1], refs[-1]
+    codes, (out_ref, stage, sem) = refs[:-3], refs[-3:]
     local, cols = codes[0].shape[1:]
-    rows = groups * prows
     space, device = where_ref[0], where_ref[1]
     share = 8 // prows
     some = 16 if local % 16 == 0 else 8
+    copies = []
 
     for tile_at in range(0, groups, share):
         t = position_of(tile_at ^ device, space, groups) // share
@@ -385,8 +385,14 @@
                         tile.append(decode(value))
                 tile = jnp.swapaxes(jnp.stack(tile), 0, 1)
                 for k in range(some):
-                    start = pl.multiple_of((at + k) * rows + t * 8, 8)
-                    out_ref[pl.ds(start, 8), lanes] = tile[k]
+                    stage[at + k, pl.ds(pl.multiple_of(t * 8, 8), 8), lanes] = tile[k]
+
+        rows_of = pl.ds(pl.multiple_of(t * 8, 8), 8)
+        copies.append(pltpu.make_async_copy(stage.at[:, rows_of, :], out_ref.at[:, rows_of, :], sem.at[len(copies)]))
+        copies[-1].start()
+
+    for copy in copies:
+        copy.wait()
 
 
 def exchange(array, axis, bit):
@@ -563,8 +569,9 @@
     out = pl.pallas_call(
         lambda *refs: last_kernel(split, groups, prows, *refs),
         in_specs=[smem] + [vmem] * (len(split) * groups),
-        out_specs=vmem,
-        out_shape=jax.ShapeDtypeStruct((local * rows, cols), f32),
+        out_specs=any_spec,
+        out_shape=jax.ShapeDtypeStruct((local, rows, cols), f32),
+        scratch_shapes=[pltpu.VMEM((local, rows, cols), f32), pltpu.SemaphoreType.DMA((groups,))],
         compiler_params=params,
         name="klast",
     )(place, *back)

time: 278 us -> 277 us (level)
  no operation moved by 1% of the time
where the time goes in v4:
time: 277 us; the launch traced here: 275 us
  waiting for transfers between devices  110 us (40%)
  starting transfers between devices  83.5 us (30%)
  Pallas kernels  69.4 us (25%)
  local copies, waits for them, and re-layouts  7.81 us (3%)
  other arithmetic  2.82 us (1%)
    ppermute x46, waiting for transfers between devices, exchange(): return lax.ppermute(array, axis, [(i, i ^ bit) for i in range(count)])  110 us
    ppermute x46, starting transfers between devices, exchange(): return lax.ppermute(array, axis, [(i, i ^ bit) for i in range(count)])  76.2 us
    pallas_call x1, Pallas kernels, body(): pl.pallas_call(lambda *refs: inner_kernel(split, sizes, plan, *refs), in_...  25.2 us
    pallas_call x1, Pallas kernels, body(): pl.pallas_call(lambda *refs: outer_two_kernel(split, sizes, plan, *refs),...  16.6 us
    pallas_call x1, Pallas kernels, body(): pl.pallas_call(lambda *refs: outer_one_kernel(split, sizes, plan, *refs),...  12.9 us
    pallas_call x1, Pallas kernels, body(): pl.pallas_call(lambda *refs: first_kernel(split, groups, prows, *refs), i...  10 us
  transfers between devices with their start and end apart: 50, of which 18 were waited for; matrix products, arithmetic and copies ran while one was open for 3% of the time, Pallas kernels for 19%

profile of v4, /device:TPU:0, one launch (start us, length us, event | category | flops | bytes accessed | tf_op | source)
XLA Modules:
  0.0 274.5 jit_solution(223220329099969)
XLA Ops:
  1.3 4.1 %collective-permute-start.18 = (bf16[1,288,256]{2,1,0:T(8,128)(2,1)S(1)}, bf16[1,288,256]{2,1,0:T(8,128)(2,1)S(1)}, u32[]{:S(2)}, u32[]{:S(2)}) collective-permute-start(bf16[1,288,256]{2,1,0:T(8,128)(2,1)S(1)} %bitcast.35), channel_id=1, source_target_pairs={{0,4},{1,5},{2,6},{3,7},{4,0},{5,1},{6,2},{7,3},{8,12},{9,13},{10,... | collective-permute-start | bytes 442376 | tf_op jit(solution)/shard_map/ppermute | solution.py:400
  12.8 6.8 %collective-permute-done = bf16[1,72,1152]{2,1,0:T(8,128)(2,1)S(1)} collective-permute-done((bf16[1,72,1152]{2,1,0:T(8,128)(2,1)S(1)}, bf16[1,72,1152]{2,1,0:T(8,128)(2,1)S(1)}, u32[]{:S(2)}, u32[]{:S(2)}) %collective-permute-start) | collective-permute-done | bytes 165920 | tf_op jit(solution)/shard_map/ppermute | solution.py:400
  24.4 10.0 %kfirst.1 = (s16[2,144,256]{2,1,0:T(8,128)(2,1)}, s16[2,144,256]{2,1,0:T(8,128)(2,1)}, s16[2,144,256]{2,1,0:T(8,128)(2,1)}, s16[2,144,256]{2,1,0:T(8,128)(2,1)},...) custom-call(s32[2]{0:T(128)} %pad_add_fusion.refs_0_, ...), custom_call_target="tpu_custom_call" | custom-call | tf_op jit(solution)/shard_map/kfirst/pallas_call | solution.py:505
  50.7 6.7 %collective-permute-done.9.refs_8_ = s16[2,144,256]{2,1,0:T(8,128)(2,1)S(1)} collective-permute-done((s16[2,144,256]{2,1,0:T(8,128)(2,1)}, s16[2,144,256]{2,1,0:T(8,128)(2,1)S(1)}, u32[]{:S(2)}, u32[]{:S(2)}) %collective-permute-start.9) | collective-permute-done | bytes 147488 | tf_op jit(solution)/shard_map/ppermute | solution.py:400
  60.4 4.2 %collective-permute-done.10.refs_9_ = s16[2,144,256]{2,1,0:T(8,128)(2,1)S(1)} collective-permute-done((s16[2,144,256]{2,1,0:T(8,128)(2,1)}, s16[2,144,256]{2,1,0:T(8,128)(2,1)S(1)}, u32[]{:S(2)}, u32[]{:S(2)}) %collective-permute-start.10) | collective-permute-done | bytes 147488 | tf_op jit(solution)/shard_map/ppermute | solution.py:400
  64.6 4.3 %collective-permute-start.11 = (s16[2,144,256]{2,1,0:T(8,128)(2,1)}, s16[2,144,256]{2,1,0:T(8,128)(2,1)}, u32[]{:S(2)}, u32[]{:S(2)}) collective-permute-start(s16[2,144,256]{2,1,0:T(8,128)(2,1)} %get-tuple-element.48), channel_id=1, source_target_pairs={{0,7},{1,6},{2,5},{3,4},{4,3},{5,2},{6,1},{7,0},{8,15},{9,14},{10,... | collective-permute-start | bytes 442376 | tf_op jit(solution)/shard_map/ppermute | solution.py:400
  68.9 3.9 %collective-permute-done.11.refs_10_ = s16[2,144,256]{2,1,0:T(8,128)(2,1)} collective-permute-done((s16[2,144,256]{2,1,0:T(8,128)(2,1)}, s16[2,144,256]{2,1,0:T(8,128)(2,1)}, u32[]{:S(2)}, u32[]{:S(2)}) %collective-permute-start.11) | collective-permute-done | bytes 147488 | tf_op jit(solution)/shard_map/ppermute | solution.py:400
  78.5 12.4 %collective-permute-done.12.refs_13_.refs_17_.refs_12_ = bf16[4,72,1152]{2,1,0:T(8,128)(2,1)} collective-permute-done((bf16[4,72,1152]{2,1,0:T(8,128)(2,1)S(1)}, bf16[4,72,1152]{2,1,0:T(8,128)(2,1)}, u32[]{:S(2)}, u32[]{:S(2)}) %collective-permute-start.12) | collective-permute-done | bytes 663584 | tf_op jit(solution)/shard_map/ppermute | solution.py:400
  91.3 25.8 %collective-permute-done.22.refs_22_.refs_26_.refs_21_ = bf16[4,288,256]{2,1,0:T(8,128)(2,1)} collective-permute-done((bf16[4,288,256]{2,1,0:T(8,128)(2,1)}, bf16[4,288,256]{2,1,0:T(8,128)(2,1)}, u32[]{:S(2)}, u32[]{:S(2)}) %collective-permute-start.22) | collective-permute-done | bytes 589856 | tf_op jit(solution)/shard_map/ppermute | solution.py:400
  120.5 12.9 %kone0.1 = (f32[2,1152,256]{2,1,0:T(8,128)}, s16[1152,256]{1,0:T(8,128)(2,1)}, s16[1152,256]{1,0:T(8,128)(2,1)}) custom-call(s32[2]{0:T(128)} %pad_add_fusion.refs_0_, f32[2,32]{1,0:T(2,128)} %concatenate.23.refs_1_, f32[2,72,128]{2,1,0:T(8,128)} %constant.24.clone.refs_2_, s16[2,144,256]{2,1,0:T(8,128)(2,1)} %get-tuple-element.41.refs_3_, ...), custom_call_target="tpu_custom_call" | custom-call | tf_op jit(solution)/shard_map/kone0/pallas_call | solution.py:525
  133.4 3.1 %collective-permute-start.34 = (s16[1152,256]{1,0:T(8,128)(2,1)}, s16[1152,256]{1,0:T(8,128)(2,1)S(1)}, u32[]{:S(2)}, u32[]{:S(2)}) collective-permute-start(s16[1152,256]{1,0:T(8,128)(2,1)} %get-tuple-element.59), channel_id=1, source_target_pairs={{0,1},{1,3},{3,2},{2,4},{4,5},{5,7},{7,6},{6,14},{14,15},{15,13},{... | collective-permute-start | bytes 1769480 | tf_op jit(solution)/shard_map/ppermute | solution.py:541
  140.0 4.0 %collective-permute-start.28 = (s16[2,144,256]{2,1,0:T(8,128)(2,1)S(1)}, s16[2,144,256]{2,1,0:T(8,128)(2,1)S(1)}, u32[]{:S(2)}, u32[]{:S(2)}) collective-permute-start(s16[2,144,256]{2,1,0:T(8,128)(2,1)S(1)} %copy-done.37), channel_id=1, source_target_pairs={{0,2},{1,3},{2,0},{3,1},{4,6},{5,7},{6,4},{7,5},{8,10},{9,11},{10,... | collective-permute-start | bytes 442376 | tf_op jit(solution)/shard_map/ppermute | solution.py:400
  144.1 11.8 %collective-permute-done.27.refs_8_ = s16[2,144,256]{2,1,0:T(8,128)(2,1)S(1)} collective-permute-done((s16[2,144,256]{2,1,0:T(8,128)(2,1)S(1)}, s16[2,144,256]{2,1,0:T(8,128)(2,1)S(1)}, u32[]{:S(2)}, u32[]{:S(2)}) %collective-permute-start.27) | collective-permute-done | bytes 147488 | tf_op jit(solution)/shard_map/ppermute | solution.py:400
  160.8 11.6 %collective-permute-done.30.refs_11_ = s16[2,144,256]{2,1,0:T(8,128)(2,1)S(1)} collective-permute-done((s16[2,144,256]{2,1,0:T(8,128)(2,1)}, s16[2,144,256]{2,1,0:T(8,128)(2,1)S(1)}, u32[]{:S(2)}, u32[]{:S(2)}) %collective-permute-start.30) | collective-permute-done | bytes 147488 | tf_op jit(solution)/shard_map/ppermute | solution.py:400
  173.6 3.6 %collective-permute-done.31.refs_12_ = s16[2,144,256]{2,1,0:T(8,128)(2,1)S(1)} collective-permute-done((s16[2,144,256]{2,1,0:T(8,128)(2,1)}, s16[2,144,256]{2,1,0:T(8,128)(2,1)S(1)}, u32[]{:S(2)}, u32[]{:S(2)}) %collective-permute-start.31) | collective-permute-done | bytes 147488 | tf_op jit(solution)/shard_map/ppermute | solution.py:400
  177.2 3.3 %collective-permute-done.33.refs_14_ = s16[2,144,256]{2,1,0:T(8,128)(2,1)S(1)} collective-permute-done((s16[2,144,256]{2,1,0:T(8,128)(2,1)}, s16[2,144,256]{2,1,0:T(8,128)(2,1)S(1)}, u32[]{:S(2)}, u32[]{:S(2)}) %collective-permute-start.33) | collective-permute-done | bytes 147488 | tf_op jit(solution)/shard_map/ppermute | solution.py:400
  181.2 25.2 %kmid.1 = (f32[2,1152,256]{2,1,0:T(8,128)}, s16[2,144,256]{2,1,0:T(8,128)(2,1)}, s16[2,144,256]{2,1,0:T(8,128)(2,1)}, s16[2,144,256]{2,1,0:T(8,128)(2,1)}, s16[2...) custom-call(s32[2]{0:T(128)} %pad_add_fusion.refs_0_, ...), custom_call_target="tpu_custom_call" | custom-call | tf_op jit(solution)/shard_map/kmid/pallas_call | solution.py:547
  208.7 3.9 %collective-permute-start.44 = (s16[2,144,256]{2,1,0:T(8,128)(2,1)}, s16[2,144,256]{2,1,0:T(8,128)(2,1)S(1)}, u32[]{:S(2)}, u32[]{:S(2)}) collective-permute-start(s16[2,144,256]{2,1,0:T(8,128)(2,1)} %get-tuple-element.71), channel_id=1, source_target_pairs={{0,2},{1,3},{2,0},{3,1},{4,6},{5,7},{6,4},{7,5},{8,10},{9,11},{10,... | collective-permute-start | bytes 442376 | tf_op jit(solution)/shard_map/ppermute | solution.py:400
  217.2 16.6 %ktwo0.1 = (s16[2,144,256]{2,1,0:T(8,128)(2,1)}, s16[2,144,256]{2,1,0:T(8,128)(2,1)}, s16[2,144,256]{2,1,0:T(8,128)(2,1)}, s16[2,144,256]{2,1,0:T(8,128)(2,1)}, ...) custom-call(s32[2]{0:T(128)} %pad_add_fusion.refs_0_, ...), custom_call_target="tpu_custom_call" | custom-call | tf_op jit(solution)/shard_map/ktwo0/pallas_call | solution.py:558
  242.5 5.4 %collective-permute-start.39 = (s16[2,144,256]{2,1,0:T(8,128)(2,1)}, s16[2,144,256]{2,1,0:T(8,128)(2,1)S(1)}, u32[]{:S(2)}, u32[]{:S(2)}) collective-permute-start(s16[2,144,256]{2,1,0:T(8,128)(2,1)} %get-tuple-element.65), channel_id=1, source_target_pairs={{0,4},{1,5},{2,6},{3,7},{4,0},{5,1},{6,2},{7,3},{8,12},{9,13},{10,... | collective-permute-start | bytes 442376 | tf_op jit(solution)/shard_map/ppermute | solution.py:400
  247.9 5.6 %collective-permute-start.40 = (s16[2,144,256]{2,1,0:T(8,128)(2,1)}, s16[2,144,256]{2,1,0:T(8,128)(2,1)S(1)}, u32[]{:S(2)}, u32[]{:S(2)}) collective-permute-start(s16[2,144,256]{2,1,0:T(8,128)(2,1)} %get-tuple-element.66), channel_id=1, source_target_pairs={{0,5},{1,4},{2,7},{3,6},{4,1},{5,0},{6,3},{7,2},{8,13},{9,12},{10,... | collective-permute-start | bytes 442376 | tf_op jit(solution)/shard_map/ppermute | solution.py:400
  257.2 8.0 %collective-permute-done.39.refs_5_ = s16[2,144,256]{2,1,0:T(8,128)(2,1)S(1)} collective-permute-done((s16[2,144,256]{2,1,0:T(8,128)(2,1)}, s16[2,144,256]{2,1,0:T(8,128)(2,1)S(1)}, u32[]{:S(2)}, u32[]{:S(2)}) %collective-permute-start.39) | collective-permute-done | bytes 147488 | tf_op jit(solution)/shard_map/ppermute | solution.py:400
  265.2 3.6 %collective-permute-done.40.refs_6_ = s16[2,144,256]{2,1,0:T(8,128)(2,1)S(1)} collective-permute-done((s16[2,144,256]{2,1,0:T(8,128)(2,1)}, s16[2,144,256]{2,1,0:T(8,128)(2,1)S(1)}, u32[]{:S(2)}, u32[]{:S(2)}) %collective-permute-start.40) | collective-permute-done | bytes 147488 | tf_op jit(solution)/shard_map/ppermute | solution.py:400
  269.6 4.7 %klast.1 = f32[144,32,256]{2,1,0:T(8,128)} custom-call(s32[2]{0:T(128)} %pad_add_fusion.refs_0_, s16[2,144,256]{2,1,0:T(8,128)(2,1)} %get-tuple-element.61.refs_1_, s16[2,144,256]{2,1,0:T(8,128)(2,1)} %copy-done.15, s16[2,144,256]{2,1,0:T(8,128)(2,1)} %copy-done.16, s16[2,144,256]{2,1,0:T(8,128)(2,1)} %copy-done.17, s16[2,144,256]{2,1,0:T(8,128)(2,1)} %copy-done.18, ...), custom_call_target="tpu_custom_call" | custom-call | tf_op jit(solution)/shard_map/klast/pallas_call | solution.py:569
  (188 shorter events, 72.0 us)
Async XLA Ops:
  1.3 20.3 %collective-permute-start.18 = (bf16[1,288,256]{2,1,0:T(8,128)(2,1)S(1)}, bf16[1,288,256]{2,1,0:T(8,128)(2,1)S(1)}, u32[]{:S(2)}, u32[]{:S(2)}) collective-permute-start(bf16[1,288,256]{2,1,0:T(8,128)(2,1)S(1)} %bitcast.35), channel_id=1, source_target_pairs={{0,4},{1,5},{2,6},{3,7},{4,0},{5,1},{6,2},{7,3},{8,12},{9,13},{10,... | collective-permute-start | bytes 442376 | tf_op jit(solution)/shard_map/ppermute | solution.py:400
  19.6 18.3 %collective-permute-start.1 = (bf16[2,72,1152]{2,1,0:T(8,128)(2,1)S(1)}, bf16[2,72,1152]{2,1,0:T(8,128)(2,1)S(1)}, u32[]{:S(2)}, u32[]{:S(2)}) collective-permute-start(bf16[2,72,1152]{2,1,0:T(8,128)(2,1)S(1)} %pad_maximum_fusion.2), channel_id=1, source_target_pairs={{0,2},{1,3},{2,0},{3,1},{4,6},{5,7},{6,4},{7,5},{8,10},{9,11},{10,... | collective-permute-start | bytes 995336 | tf_op jit(solution)/shard_map/ppermute | solution.py:400
  21.7 18.5 %collective-permute-start.19 = (bf16[2,288,256]{2,1,0:T(8,128)(2,1)S(1)}, bf16[2,288,256]{2,1,0:T(8,128)(2,1)S(1)}, u32[]{:S(2)}, u32[]{:S(2)}) collective-permute-start(bf16[2,288,256]{2,1,0:T(8,128)(2,1)S(1)} %pad_maximum_fusion.3), channel_id=1, source_target_pairs={{0,2},{1,3},{2,0},{3,1},{4,6},{5,7},{6,4},{7,5},{8,10},{9,11},{10,... | collective-permute-start | bytes 884744 | tf_op jit(solution)/shard_map/ppermute | solution.py:400
  40.2 34.2 %collective-permute-start.2 = (bf16[4,72,1152]{2,1,0:T(8,128)(2,1)S(1)}, bf16[4,72,1152]{2,1,0:T(8,128)(2,1)S(1)}, u32[]{:S(2)}, u32[]{:S(2)}) collective-permute-start(bf16[4,72,1152]{2,1,0:T(8,128)(2,1)S(1)} %pad_maximum_fusion.refs_11_.refs_15_.refs_10_), channel_id=1, source_target_pairs={{0,1},{1,0},{2,3},{3,2},{4,5},{5,4},{6,7},{7,6},{8,9},{9,8},{10,11... | collective-permute-start | bytes 1990664 | tf_op jit(solution)/shard_map/ppermute | solution.py:400
  41.8 31.0 %collective-permute-start.23 = (bf16[4,288,256]{2,1,0:T(8,128)(2,1)S(1)}, bf16[4,288,256]{2,1,0:T(8,128)(2,1)S(1)}, u32[]{:S(2)}, u32[]{:S(2)}) collective-permute-start(bf16[4,288,256]{2,1,0:T(8,128)(2,1)S(1)} %pad_maximum_fusion.1.refs_19_.refs_23_.refs_18_), channel_id=1, source_target_pairs={{0,8},{8,0},{16,24},{24,16},{1,9},{9,1},{17,25},{25,17},{2,10},{10... | collective-permute-start | bytes 1769480 | tf_op jit(solution)/shard_map/ppermute | solution.py:400
  44.9 30.0 %collective-permute-start.21 = (bf16[4,288,256]{2,1,0:T(8,128)(2,1)S(1)}, bf16[4,288,256]{2,1,0:T(8,128)(2,1)}, u32[]{:S(2)}, u32[]{:S(2)}) collective-permute-start(bf16[4,288,256]{2,1,0:T(8,128)(2,1)S(1)} %pad_maximum_fusion.1.refs_19_.refs_23_.refs_18_), channel_id=1, source_target_pairs={{0,16},{8,24},{16,0},{24,8},{1,17},{9,25},{17,1},{25,9},{2,18},{10... | collective-permute-start | bytes 1769480 | tf_op jit(solution)/shard_map/ppermute | solution.py:400
  47.3 29.5 %collective-permute-start.20 = (bf16[4,288,256]{2,1,0:T(8,128)(2,1)S(1)}, bf16[4,288,256]{2,1,0:T(8,128)(2,1)}, u32[]{:S(2)}, u32[]{:S(2)}) collective-permute-start(bf16[4,288,256]{2,1,0:T(8,128)(2,1)S(1)} %pad_maximum_fusion.1.refs_19_.refs_23_.refs_18_), channel_id=1, source_target_pairs={{0,1},{1,0},{2,3},{3,2},{4,5},{5,4},{6,7},{7,6},{8,9},{9,8},{10,11... | collective-permute-start | bytes 1769480 | tf_op jit(solution)/shard_map/ppermute | solution.py:400
  74.4 42.7 %collective-permute-start.13 = (bf16[4,72,1152]{2,1,0:T(8,128)(2,1)S(1)}, bf16[4,72,1152]{2,1,0:T(8,128)(2,1)}, u32[]{:S(2)}, u32[]{:S(2)}) collective-permute-start(bf16[4,72,1152]{2,1,0:T(8,128)(2,1)S(1)} %collective-permute-done.2.refs_12_.refs_16_.refs_11_), channel_id=1, source_target_pairs={{0,16},{8,24},{16,0},{24,8},{1,17},{9,25},{17,1},{25,9},{2,18},{10... | collective-permute-start | bytes 1990664 | tf_op jit(solution)/shard_map/ppermute | solution.py:400
  76.8 40.3 %collective-permute-start.22 = (bf16[4,288,256]{2,1,0:T(8,128)(2,1)}, bf16[4,288,256]{2,1,0:T(8,128)(2,1)}, u32[]{:S(2)}, u32[]{:S(2)}) collective-permute-start(bf16[4,288,256]{2,1,0:T(8,128)(2,1)} %collective-permute-done.20.refs_20_.refs_24_.refs_19_), channel_id=1, source_target_pairs={{0,16},{8,24},{16,0},{24,8},{1,17},{9,25},{17,1},{25,9},{2,18},{10... | collective-permute-start | bytes 1769480 | tf_op jit(solution)/shard_map/ppermute | solution.py:400
  78.4 40.0 %collective-permute-start.24 = (bf16[4,288,256]{2,1,0:T(8,128)(2,1)}, bf16[4,288,256]{2,1,0:T(8,128)(2,1)}, u32[]{:S(2)}, u32[]{:S(2)}) collective-permute-start(bf16[4,288,256]{2,1,0:T(8,128)(2,1)} %collective-permute-done.20.refs_20_.refs_24_.refs_19_), channel_id=1, source_target_pairs={{0,8},{8,0},{16,24},{24,16},{1,9},{9,1},{17,25},{25,17},{2,10},{10... | collective-permute-start | bytes 1769480 | tf_op jit(solution)/shard_map/ppermute | solution.py:400
  90.8 27.6 %collective-permute-start.15 = (bf16[4,72,1152]{2,1,0:T(8,128)(2,1)S(1)}, bf16[4,72,1152]{2,1,0:T(8,128)(2,1)}, u32[]{:S(2)}, u32[]{:S(2)}) collective-permute-start(bf16[4,72,1152]{2,1,0:T(8,128)(2,1)S(1)} %collective-permute-done.2.refs_12_.refs_16_.refs_11_), channel_id=1, source_target_pairs={{0,8},{8,0},{16,24},{24,16},{1,9},{9,1},{17,25},{25,17},{2,10},{10... | collective-permute-start | bytes 1990664 | tf_op jit(solution)/shard_map/ppermute | solution.py:400
  90.8 27.6 %collective-permute-start.16 = (bf16[4,72,1152]{2,1,0:T(8,128)(2,1)}, bf16[4,72,1152]{2,1,0:T(8,128)(2,1)}, u32[]{:S(2)}, u32[]{:S(2)}) collective-permute-start(bf16[4,72,1152]{2,1,0:T(8,128)(2,1)} %collective-permute-done.12.refs_13_.refs_17_.refs_12_), channel_id=1, source_target_pairs={{0,8},{8,0},{16,24},{24,16},{1,9},{9,1},{17,25},{25,17},{2,10},{10... | collective-permute-start | bytes 1990664 | tf_op jit(solution)/shard_map/ppermute | solution.py:400
  133.4 79.7 %collective-permute-start.34 = (s16[1152,256]{1,0:T(8,128)(2,1)}, s16[1152,256]{1,0:T(8,128)(2,1)S(1)}, u32[]{:S(2)}, u32[]{:S(2)}) collective-permute-start(s16[1152,256]{1,0:T(8,128)(2,1)} %get-tuple-element.59), channel_id=1, source_target_pairs={{0,1},{1,3},{3,2},{2,4},{4,5},{5,7},{7,6},{6,14},{14,15},{15,13},{... | collective-permute-start | bytes 1769480 | tf_op jit(solution)/shard_map/ppermute | solution.py:541
  136.5 19.4 %collective-permute-start.27 = (s16[2,144,256]{2,1,0:T(8,128)(2,1)S(1)}, s16[2,144,256]{2,1,0:T(8,128)(2,1)S(1)}, u32[]{:S(2)}, u32[]{:S(2)}) collective-permute-start(s16[2,144,256]{2,1,0:T(8,128)(2,1)S(1)} %copy-done.38), channel_id=1, source_target_pairs={{0,1},{1,0},{2,3},{3,2},{4,5},{5,4},{6,7},{7,6},{8,9},{9,8},{10,11... | collective-permute-start | bytes 442376 | tf_op jit(solution)/shard_map/ppermute | solution.py:400
  138.5 77.2 %collective-permute-start.35 = (s16[1152,256]{1,0:T(8,128)(2,1)}, s16[1152,256]{1,0:T(8,128)(2,1)S(1)}, u32[]{:S(2)}, u32[]{:S(2)}) collective-permute-start(s16[1152,256]{1,0:T(8,128)(2,1)} %get-tuple-element.60), channel_id=1, source_target_pairs={{1,0},{3,1},{2,3},{4,2},{5,4},{7,5},{6,7},{14,6},{15,14},{13,15},{... | collective-permute-start | bytes 1769480 | tf_op jit(solution)/shard_map/ppermute | solution.py:542
  140.0 18.7 %collective-permute-start.28 = (s16[2,144,256]{2,1,0:T(8,128)(2,1)S(1)}, s16[2,144,256]{2,1,0:T(8,128)(2,1)S(1)}, u32[]{:S(2)}, u32[]{:S(2)}) collective-permute-start(s16[2,144,256]{2,1,0:T(8,128)(2,1)S(1)} %copy-done.37), channel_id=1, source_target_pairs={{0,2},{1,3},{2,0},{3,1},{4,6},{5,7},{6,4},{7,5},{8,10},{9,11},{10,... | collective-permute-start | bytes 442376 | tf_op jit(solution)/shard_map/ppermute | solution.py:400
  158.6 18.6 %collective-permute-start.31 = (s16[2,144,256]{2,1,0:T(8,128)(2,1)}, s16[2,144,256]{2,1,0:T(8,128)(2,1)S(1)}, u32[]{:S(2)}, u32[]{:S(2)}) collective-permute-start(s16[2,144,256]{2,1,0:T(8,128)(2,1)} %get-tuple-element.55), channel_id=1, source_target_pairs={{0,5},{1,4},{2,7},{3,6},{4,1},{5,0},{6,3},{7,2},{8,13},{9,12},{10,... | collective-permute-start | bytes 442376 | tf_op jit(solution)/shard_map/ppermute | solution.py:400
  206.4 27.5 %collective-permute-start.43 = (s16[2,144,256]{2,1,0:T(8,128)(2,1)}, s16[2,144,256]{2,1,0:T(8,128)(2,1)S(1)}, u32[]{:S(2)}, u32[]{:S(2)}) collective-permute-start(s16[2,144,256]{2,1,0:T(8,128)(2,1)} %get-tuple-element.70), channel_id=1, source_target_pairs={{0,1},{1,0},{2,3},{3,2},{4,5},{5,4},{6,7},{7,6},{8,9},{9,8},{10,11... | collective-permute-start | bytes 442376 | tf_op jit(solution)/shard_map/ppermute | solution.py:400
  208.7 27.5 %collective-permute-start.44 = (s16[2,144,256]{2,1,0:T(8,128)(2,1)}, s16[2,144,256]{2,1,0:T(8,128)(2,1)S(1)}, u32[]{:S(2)}, u32[]{:S(2)}) collective-permute-start(s16[2,144,256]{2,1,0:T(8,128)(2,1)} %get-tuple-element.71), channel_id=1, source_target_pairs={{0,2},{1,3},{2,0},{3,1},{4,6},{5,7},{6,4},{7,5},{8,10},{9,11},{10,... | collective-permute-start | bytes 442376 | tf_op jit(solution)/shard_map/ppermute | solution.py:400
  212.7 25.9 %collective-permute-start.45 = (s16[2,144,256]{2,1,0:T(8,128)(2,1)}, s16[2,144,256]{2,1,0:T(8,128)(2,1)S(1)}, u32[]{:S(2)}, u32[]{:S(2)}) collective-permute-start(s16[2,144,256]{2,1,0:T(8,128)(2,1)} %get-tuple-element.72), channel_id=1, source_target_pairs={{0,3},{1,2},{2,1},{3,0},{4,7},{5,6},{6,5},{7,4},{8,11},{9,10},{10,... | collective-permute-start | bytes 442376 | tf_op jit(solution)/shard_map/ppermute | solution.py:400
  213.1 26.2 %collective-permute-start.46 = (s16[2,144,256]{2,1,0:T(8,128)(2,1)}, s16[2,144,256]{2,1,0:T(8,128)(2,1)S(1)}, u32[]{:S(2)}, u32[]{:S(2)}) collective-permute-start(s16[2,144,256]{2,1,0:T(8,128)(2,1)} %get-tuple-element.73), channel_id=1, source_target_pairs={{0,4},{1,5},{2,6},{3,7},{4,0},{5,1},{6,2},{7,3},{8,12},{9,13},{10,... | collective-permute-start | bytes 442376 | tf_op jit(solution)/shard_map/ppermute | solution.py:400
  215.7 23.6 %collective-permute-start.47 = (s16[2,144,256]{2,1,0:T(8,128)(2,1)}, s16[2,144,256]{2,1,0:T(8,128)(2,1)S(1)}, u32[]{:S(2)}, u32[]{:S(2)}) collective-permute-start(s16[2,144,256]{2,1,0:T(8,128)(2,1)} %get-tuple-element.74), channel_id=1, source_target_pairs={{0,5},{1,4},{2,7},{3,6},{4,1},{5,0},{6,3},{7,2},{8,13},{9,12},{10,... | collective-permute-start | bytes 442376 | tf_op jit(solution)/shard_map/ppermute | solution.py:400
  242.5 22.7 %collective-permute-start.39 = (s16[2,144,256]{2,1,0:T(8,128)(2,1)}, s16[2,144,256]{2,1,0:T(8,128)(2,1)S(1)}, u32[]{:S(2)}, u32[]{:S(2)}) collective-permute-start(s16[2,144,256]{2,1,0:T(8,128)(2,1)} %get-tuple-element.65), channel_id=1, source_target_pairs={{0,4},{1,5},{2,6},{3,7},{4,0},{5,1},{6,2},{7,3},{8,12},{9,13},{10,... | collective-permute-start | bytes 442376 | tf_op jit(solution)/shard_map/ppermute | solution.py:400
  247.9 20.9 %collective-permute-start.40 = (s16[2,144,256]{2,1,0:T(8,128)(2,1)}, s16[2,144,256]{2,1,0:T(8,128)(2,1)S(1)}, u32[]{:S(2)}, u32[]{:S(2)}) collective-permute-start(s16[2,144,256]{2,1,0:T(8,128)(2,1)} %get-tuple-element.66), channel_id=1, source_target_pairs={{0,5},{1,4},{2,7},{3,6},{4,1},{5,0},{6,3},{7,2},{8,13},{9,12},{10,... | collective-permute-start | bytes 442376 | tf_op jit(solution)/shard_map/ppermute | solution.py:400
  (67 other events, 1195.4 us)
